TPU v7x, 32 devices: a whole 2x2x4 slice. The times are simulated.
32 devices in a mesh: sec: 4 (over x, core), swath: 8 (over z, y).
Axes of the slice: x: 2, y: 2, z: 4, core: 2. Of those that a mesh axis runs over, the one named last changes fastest.
Arguments:
- radar_l: bfloat16 [6, 1536, 1024], P(None, 'sec', 'swath'), may hold values from -6 to 6
- radar_s: bfloat16 [6, 1024, 1024], P(None, 'sec', 'swath'), may hold values from -6 to 6
- weights_l: bfloat16 [12288, 128, 128], P(('sec', 'swath')), may hold values from -0.5 to 0.5
- weights_s: bfloat16 [8192, 128, 128], P(('sec', 'swath')), may hold values from -0.5 to 0.5
- owner_l: int32 [12288, 1], P(('sec', 'swath')), may hold values from 0 to 31; in each aligned block of 384 rows (0 to 383, 384 to 767, ...) at most 24 rows name the same one
- owner_s: int32 [8192, 1], P(('sec', 'swath')), may hold values from 0 to 31; in each aligned block of 256 rows (0 to 255, 256 to 511, ...) at most 16 rows name the same one
- slot_l: int32 [12288], P(('sec', 'swath')), may hold values from 0 to 255
- slot_s: int32 [8192], P(('sec', 'swath')), may hold values from 0 to 255
- models: float32 [16, 36], replicated, may hold values from -1 to 1
Outputs:
- fit: float32 [16, 1024, 1024], P(None, 'sec', 'swath')
Inputs may be any that keep to these rules, and one draw needn't show every extreme that they name: `owner_l`: within the tiles of one device, each owner is named by at most 24 tiles. `owner_s`: within the tiles of one device, each owner is named by at most 16 tiles.
All inputs are finite; a program needn't handle non-finite values.
Results may differ from a plain program's by a relative error of at most 0.0038.
Values may be sent and summed in bfloat16 or wider, within the bound.
No kernel may reach another device: no remote copies, remote signals or barrier semaphores. Data moves between devices by JAX's collectives and lax.ppermute only.
A program may use at most 192 MiB of HBM per device.

v0:
```python
import jax
import jax.numpy as jnp
from jax import lax
from jax.experimental import pallas as pl
from jax.experimental.pallas import tpu as pltpu
from jax.sharding import PartitionSpec as P

FIT_ITERS = 4
AXES = ("sec", "swath")

cu_square = 0.25
fit_rate = 0.25
upper_pairs = [(first, second) for first in range(6) for second in range(first, 6)]
strict_pairs = [(first, second) for first in range(6) for second in range(first + 1, 6)]
CHANNELS = len(upper_pairs) + len(strict_pairs)
COMPS = 6
NT = (((1,), (1,)), ((), ()))
NN = (((1,), (0,)), ((), ()))
TN = (((0,), (0,)), ((), ()))
HI = lax.Precision.HIGHEST
F32 = jnp.float32
BF16 = jnp.bfloat16
SUB = 8
LANES = 128
EXTRA = 5


def params(mib):
    return pltpu.CompilerParams(vmem_limit_bytes=mib << 20)


def iota(shape, dim):
    return lax.broadcasted_iota(jnp.int32, shape, dim)


def dot(a, b, dims, precision=None):
    return lax.dot_general(a, b, dims, precision=precision, preferred_element_type=F32)


def ones_where(mask, dtype=BF16):
    return jnp.where(mask, 1.0, 0.0).astype(dtype)


def exchange(first, last, axis):
    peers = lax.axis_size(axis)
    up = [(i, i + 1) for i in range(peers - 1)]
    down = [(j, i) for i, j in up]
    return lax.ppermute(last, axis, up), lax.ppermute(first, axis, down)


VMEM = pl.BlockSpec(memory_space=pltpu.VMEM)
SMEM = pl.BlockSpec(memory_space=pltpu.SMEM)


def up_to(n, multiple):
    return -(-n // multiple) * multiple


class Sizes:
    def __init__(self, lines_l, map_lines, n_model):
        self.devices = lax.axis_size(AXES)
        self.swath = lax.axis_size("swath")
        self.lines = (lines_l, map_lines)
        self.map_lines = map_lines
        self.n_model = n_model
        self.caps = tuple(max(2, 2 * lines // self.devices) for lines in self.lines)
        self.starts = (0, COMPS * self.caps[0])
        self.rows = up_to(COMPS * sum(self.caps), SUB)
        self.stride = up_to(self.rows + SUB, LANES)
        self.lanes = up_to(self.rows, LANES)


def first_kernel(z, radar_l, radar_s, owner_l, slot_l, owner_s, slot_s, first, last, base_l, base_s, marks):
    wide = COMPS * LANES
    pick = iota((2 * SUB, wide), 1) == jnp.where(
        iota((2 * SUB, wide), 0) < SUB,
        iota((2 * SUB, wide), 0) * LANES,
        (iota((2 * SUB, wide), 0) - SUB) * LANES + LANES - 1,
    )
    pick = ones_where(pick)
    at = 0
    for radar, lines in ((radar_l, z.lines[0]), (radar_s, z.lines[1])):
        rows = jnp.concatenate([radar[c] for c in range(COMPS)], axis=1)
        both = dot(pick, rows, NT)
        first[:, at : at + lines] = both[0:SUB].astype(BF16)
        last[:, at : at + lines] = both[SUB:].astype(BF16)
        at += lines
    total = jnp.zeros((z.devices, LANES), F32)
    shift = 0
    for band, (owner, slot, base) in enumerate(((owner_l, slot_l, base_l), (owner_s, slot_s, base_s))):
        tiles = z.lines[band]
        hit = iota((z.devices, tiles), 0) == owner[...]
        earlier = ones_where(iota((tiles, tiles), 0) < iota((tiles, tiles), 1))
        before = dot(ones_where(hit), earlier, NN)
        rank = jnp.sum(jnp.where(hit, before, 0.0), axis=0, keepdims=True).astype(jnp.int32)
        base[...] = owner[...] * z.stride + z.starts[band] + rank
        line = jnp.where(hit, slot[...] + 1, 0).astype(F32).astype(BF16)
        place = ones_where(iota((LANES, tiles), 0) == rank + shift)
        total = total + dot(line, place, NT)
        shift += z.caps[band]
    me, other = iota((z.devices, z.devices), 0), iota((z.devices, z.devices), 1)
    swath = z.swath
    inner = iota((z.devices, z.devices), 0) % swath
    own = total.astype(BF16)
    before = dot(ones_where((other == me - 1) & (inner > 0)), own, NN)
    after = dot(ones_where((other == me + 1) & (inner < swath - 1)), own, NN)
    marks[...] = total + pltpu.roll(before, shift, 1) + pltpu.roll(after, 2 * shift, 1)


def second_kernel(z, top_l, top_s, bottom_l, bottom_s, before, after, first, last):
    lines_l, lines_s = z.lines
    ends = (
        (first, top_l, top_s, 0, 0, lines_l),
        (last, bottom_l, bottom_s, top_l.shape[1] - 1, lines_l - 1, lines_l + lines_s - 1),
    )
    for out, rows_l, rows_s, row, at_l, at_s in ends:
        parts = [rows_l[...].astype(F32)[:, row, :], rows_s[...].astype(F32)[:, row, :]]
        for side in (before, after):
            for at in (at_l, at_s):
                tile = at // LANES * LANES
                column = side[:, tile : tile + LANES].astype(F32)[0:COMPS, at - tile : at - tile + 1]
                parts.append(jnp.broadcast_to(column, (COMPS, LANES)))
        parts.append(jnp.zeros((out.shape[0] - 6 * COMPS, LANES), F32))
        out[...] = jnp.concatenate(parts, axis=0).astype(BF16)


def with_sides(x, left, right):
    lane = iota(x.shape, 1)
    width = x.shape[1]
    before = jnp.where(lane == 0, left, pltpu.roll(x, 1, 1))
    after = jnp.where(lane == width - 1, right, pltpu.roll(x, width - 1, 1))
    return before, after


def filter_band(band, tiles, radar, left, right, above, below, work, filtered):
    inner = pl.ds(SUB, tiles)
    ends = ((SUB - 1, above), (SUB + tiles, below))

    def end_values(strip, c):
        row = band * COMPS + c
        corner = 2 * COMPS + row
        return strip[row : row + 1], strip[corner : corner + 1, 0:1], strip[corner + 2 * COMPS : corner + 2 * COMPS + 1, 0:1]

    def power_of(values):
        total = [0.0, 0.0, 0.0]
        for triple in values:
            total = [t + v * v for t, v in zip(total, triple)]
        return (total[0],) + with_sides(*total)

    body = [radar[c].astype(F32) for c in range(COMPS)]
    lefts = [left[:, c : c + 1] for c in range(COMPS)]
    rights = [right[:, c : c + 1] for c in range(COMPS)]
    for plane, value in enumerate(power_of(zip(body, lefts, rights))):
        work[plane, inner, :] = value
    for row, strip in ends:
        for plane, value in enumerate(power_of([end_values(strip, c) for c in range(COMPS)])):
            work[plane, pl.ds(row, 1), :] = value
    near = [work[plane, pl.ds(SUB + d, tiles), :] for plane in range(3) for d in (-1, 0, 1)]
    mean_power = sum(near[1:], near[0]) / 9.0
    spread = jnp.zeros_like(mean_power)
    for q in near:
        spread = spread + (q - mean_power) ** 2
    spread = spread / 9.0
    gain = spread / (spread + cu_square * mean_power * mean_power + 1.0)
    for c in range(COMPS):
        plane = c % 3
        before, after = with_sides(body[c], lefts[c], rights[c])
        work[plane, inner, :] = body[c] + before + after
        for row, strip in ends:
            x, corner_left, corner_right = end_values(strip, c)
            before, after = with_sides(x, corner_left, corner_right)
            work[plane, pl.ds(row, 1), :] = x + before + after
        mean = work[plane, pl.ds(SUB - 1, tiles), :] + work[plane, inner, :]
        mean = (mean + work[plane, pl.ds(SUB + 1, tiles), :]) / 9.0
        filtered[pl.ds(c, tiles, stride=SUB), :] = mean + gain * (body[c] - mean)


def send_kernel(
    z, base_l, base_s, radar_l, radar_s, before, after, above, below, marks, weights_l, weights_s,
    out, work, filtered, packed, held_l, held_s, arrived,
):
    chunks = []
    for source, held, lines in ((weights_l, held_l, z.lines[0]), (weights_s, held_s, z.lines[1])):
        size = 64 if lines % 64 == 0 else lines
        copies = []
        for at in range(0, lines, size):
            part = pl.ds(at, size)
            copies.append(
                pltpu.make_async_copy(source.at[part], held.at[part], arrived.at[sum(map(len, chunks)) + len(copies)])
            )
            copies[-1].start()
        chunks.append(copies)
    packed[...] = jnp.zeros_like(packed)
    left, right = before[...].astype(F32).T, after[...].astype(F32).T
    up, down = above[...].astype(F32), below[...].astype(F32)
    at = 0
    for band, (radar, base, weights) in enumerate(
        ((radar_l, base_l, held_l), (radar_s, base_s, held_s))
    ):
        tiles, capacity = z.lines[band], z.caps[band]
        filter_band(
            band, tiles, radar, left[at : at + tiles], right[at : at + tiles], up, down, work, filtered
        )
        at += tiles

        size = tiles // len(chunks[band])
        for i, copy in enumerate(chunks[band]):
            copy.wait()
            for t in range(0, size, 2):
                tile = i * size + t
                lines = filtered[pl.ds(tile * SUB, 2 * SUB), :].astype(BF16)
                matrix = weights[pl.ds(tile, 2)].reshape(2 * LANES, LANES)
                result = dot(lines, matrix, NT)
                first, second = base[0, tile], base[0, tile + 1]
                packed[pl.ds(first, COMPS, stride=capacity), :] = result[0:COMPS, 0:LANES]
                packed[pl.ds(second, COMPS, stride=capacity), :] = result[SUB : SUB + COMPS, LANES:]

    steps = z.lanes // LANES
    row, lane = iota((SUB, LANES), 0), iota((SUB, LANES), 1)
    pick = ones_where(
        ((row >= 1) & (row <= steps) & (lane == LANES - 1)) | ((row > steps) & (row <= 2 * steps) & (lane == 0))
    )
    columns = []
    for o in range(z.devices):
        columns.append(dot(pick, packed[o * z.stride : o * z.stride + z.lanes, :].astype(BF16), NT))
    for o in range(z.devices):
        extra = jnp.broadcast_to(marks[o : o + 1, :], (SUB, LANES))
        one_less, one_more = max(o - 1, 0), min(o + 1, z.devices - 1)
        for k in range(steps):
            part = slice(k * LANES, (k + 1) * LANES)
            extra = jnp.where(row == 1 + k, columns[one_less][:, part], extra)
            extra = jnp.where(row == 1 + steps + k, columns[one_more][:, part], extra)
        packed[o * z.stride + z.rows : o * z.stride + z.rows + SUB, :] = extra
    for o in range(z.devices):
        out[o] = packed[o * z.stride : o * z.stride + z.rows + SUB, :].astype(BF16)


def matrix_kernel(models, small, wide):
    m = models[...]
    n_model = m.shape[0]
    eye = ones_where(iota((CHANNELS, CHANNELS), 0) == iota((CHANNELS, CHANNELS), 1), F32)
    powers = jnp.zeros(m.shape, F32)
    for _ in range(FIT_ITERS):
        predicted = dot(m, powers, TN, HI)
        powers = powers + fit_rate * dot(m, eye - predicted, NN, HI)
    powers = powers / 9.0
    small[...] = powers
    rows, columns = wide.shape[0], wide.shape[1] // 3
    left = ones_where(iota((rows, n_model), 0) // SUB == iota((rows, n_model), 1), F32)
    right = ones_where(iota((CHANNELS, columns), 1) // SUB == iota((CHANNELS, columns), 0), F32)
    spread = dot(dot(left, powers, NN, HI), right, NN, HI)
    same = iota((rows, columns), 0) % SUB == iota((rows, columns), 1) % SUB
    spread = jnp.where(same, spread, 0.0)
    high = spread.astype(BF16)
    low = (spread - high.astype(F32)).astype(BF16)
    wide[...] = jnp.concatenate([high, high, low], axis=1)


def coherency(real, imag):
    joint = [real[f] * real[g] + imag[f] * imag[g] for f, g in upper_pairs]
    return joint + [imag[f] * real[g] - real[f] * imag[g] for f, g in strict_pairs]


def split_parts(maps):
    pick = lambda at: [maps(band * COMPS + at + c) for band in range(2) for c in range(3)]
    return pick(0), pick(3)


def merge_kernel(z, got, small, wide, out, rim_first, rim_last, stage, extras, maps, fits):
    map_lines, n_model, devices = z.map_lines, z.n_model, z.devices
    steps = z.lanes // LANES
    for s in range(devices):
        extras[s * SUB : (s + 1) * SUB, :] = got[s, z.rows : z.rows + SUB, :].astype(F32)
    piece = lambda r: extras[pl.ds(r, devices, stride=SUB), :]
    marks = piece(0)
    sides = [
        jnp.concatenate([piece(1 + side * steps + k) for k in range(steps)], axis=1) for side in range(2)
    ]
    shift = sum(z.caps)
    edges = [[None] * (2 * COMPS) for _ in range(2)]
    at_mark = 0
    for band in range(2):
        capacity = z.caps[band]
        places = devices * capacity
        for s in range(devices):
            block = got[s, 0 : z.rows, :].astype(F32)
            for c in range(COMPS):
                low = z.starts[band] + c * capacity
                stage[s * capacity : (s + 1) * capacity, c * LANES : (c + 1) * LANES] = block[
                    low : low + capacity, :
                ]
        turned = lambda x, by: pltpu.roll(x, (x.shape[1] - by) % x.shape[1], 1)[:, 0:LANES]
        rows = [turned(marks, at_mark + k * shift) for k in range(3)]
        for side in range(2):
            rows += [turned(sides[side], z.starts[band] + c * capacity) for c in range(COMPS)]
        at_mark += capacity
        place = iota((devices, places), 1)
        low = iota((devices, places), 0) * capacity
        mine = (place >= low) & (place < low + capacity)
        offset = jnp.sum(jnp.where(mine, place - low, 0), axis=0, keepdims=True)
        pick = ones_where(iota((LANES, places), 0) == offset)
        spread = dot(jnp.concatenate(rows, axis=0).astype(BF16), pick, NN)
        flat = [
            jnp.sum(jnp.where(mine, spread[k * devices : (k + 1) * devices], 0.0), axis=0, keepdims=True)
            for k in range(len(rows))
        ]
        lines = iota((map_lines, places), 0) + 1
        tables = [ones_where(lines == flat[k].astype(jnp.int32)) for k in range(3)]
        summed = dot(tables[0], stage[0:places, :].astype(BF16), NN)
        for c in range(COMPS):
            maps[band * COMPS + c] = summed[:, c * LANES : (c + 1) * LANES]
        for side in range(2):
            values = flat[3 + side * COMPS : 3 + (side + 1) * COMPS]
            values = jnp.concatenate(values + [jnp.zeros((SUB - COMPS, places), F32)], axis=0).astype(BF16)
            column = dot(values, tables[1 + side], NT)
            for c in range(COMPS):
                edges[side][band * COMPS + c] = column[c : c + 1, :]
    turned = []
    for side in range(2):
        joint = jnp.concatenate(coherency(*split_parts(lambda i: edges[side][i])), axis=0)
        turned.append(dot(small[...], joint, NN, HI).T)

    matrix = wide[...]

    def step(i, _):
        halves = []
        for h in range(2):
            r = pl.multiple_of((2 * i + h) * SUB, SUB)
            x = jnp.concatenate(coherency(*split_parts(lambda n: maps[n, pl.ds(r, SUB), :])), axis=0)
            halves.append(x)
        x = jnp.concatenate(halves, axis=1)
        high = x.astype(BF16)
        low = (x - high.astype(F32)).astype(BF16)
        result = dot(matrix, jnp.concatenate([high, low, high], axis=0), NN)
        for h in range(2):
            r = pl.multiple_of((2 * i + h) * SUB, SUB)
            for k in range(n_model):
                fits[k, pl.ds(SUB + r, SUB), :] = result[
                    k * SUB : (k + 1) * SUB, h * LANES : (h + 1) * LANES
                ]
        return _

    lax.fori_loop(0, map_lines // (2 * SUB), step, 0)
    blank = jnp.zeros((1, LANES), F32)
    inner = pl.ds(SUB, map_lines)
    for k in range(n_model):
        x = fits[k, inner, :]
        before, after = with_sides(x, turned[0][:, k : k + 1], turned[1][:, k : k + 1])
        x = x + before + after
        fits[k, inner, :] = x
        fits[k, SUB - 1 : SUB, :] = blank
        fits[k, SUB + map_lines : SUB + map_lines + 1, :] = blank
        rim_first[k : k + 1, :] = x[0:1, :]
        rim_last[k : k + 1, :] = x[map_lines - 1 :, :]
        out[k] = fits[k, pl.ds(SUB - 1, map_lines), :] + x + fits[k, pl.ds(SUB + 1, map_lines), :]


def finish_kernel(fit, above, below, out):
    end = pl.program_id(0)
    line = iota(fit.shape[1:], 0)
    height = fit.shape[1]
    for k in range(fit.shape[0]):
        upper = jnp.where((line == 0) & (end == 0), above[k : k + 1, :], 0.0)
        lower = jnp.where((line == height - 1) & (end == 1), below[k : k + 1, :], 0.0)
        out[k] = fit[k] + upper + lower


def body(radar_l, radar_s, weights_l, weights_s, owner_l, owner_s, slot_l, slot_s, models):
    z = Sizes(radar_l.shape[1], radar_s.shape[1], models.shape[0])
    lines_l, lines_s = z.lines
    shape = jax.ShapeDtypeStruct

    def call(kernel, args, shapes, mib, scratch=(), specs=None, flops=0, size=0):
        return pl.pallas_call(
            lambda *refs: kernel(z, *refs) if kernel is not matrix_kernel else kernel(*refs),
            in_specs=specs or [VMEM] * len(args),
            out_specs=[VMEM] * len(shapes),
            out_shape=shapes,
            scratch_shapes=scratch,
            compiler_params=params(mib),
            cost_estimate=pl.CostEstimate(flops=flops, bytes_accessed=size, transcendentals=0),
        )(*args)

    row = lambda x: x.reshape(1, -1)
    column = shape((SUB, lines_l + lines_s), BF16)
    first, last, base_l, base_s, marks = call(
        first_kernel,
        (radar_l, radar_s, row(owner_l), row(slot_l), row(owner_s), row(slot_s)),
        [column, column, shape((1, lines_l), jnp.int32), shape((1, lines_s), jnp.int32), shape((z.devices, LANES), F32)],
        16, flops=30_000_000, size=2_000_000,
    )
    before, after = exchange(first, last, "swath")
    strip = shape((5 * SUB, LANES), BF16)
    tall = 2 * SUB
    edge = lambda lines, end: pl.BlockSpec(
        (COMPS, tall, LANES), lambda i: (0, end * (lines // tall - 1), 0)
    )
    side = pl.BlockSpec(before.shape, lambda i: (0, 0))
    first, last = pl.pallas_call(
        lambda *refs: second_kernel(z, *refs),
        grid=(1,),
        in_specs=[edge(lines, end) for end in range(2) for lines in z.lines] + [side, side],
        out_specs=[pl.BlockSpec(strip.shape, lambda i: (0, 0))] * 2,
        out_shape=[strip, strip],
        compiler_params=params(16),
    )(radar_l, radar_s, radar_l, radar_s, before, after)
    above, below = exchange(first, last, "sec")
    args = (base_l, base_s, radar_l, radar_s, before, after, above, below, marks, weights_l, weights_s)
    (sent,) = call(
        send_kernel,
        args,
        [shape((z.devices, z.rows + SUB, LANES), BF16)],
        44,
        specs=[SMEM, SMEM] + [VMEM] * (len(args) - 4) + [pl.BlockSpec(memory_space=pl.ANY)] * 2,
        scratch=[
            pltpu.VMEM((3, max(z.lines) + 2 * SUB, LANES), F32),
            pltpu.VMEM((max(z.lines) * SUB, LANES), F32),
            pltpu.VMEM((z.devices * z.stride + up_to(COMPS * max(z.caps), SUB), LANES), F32),
            pltpu.VMEM(weights_l.shape, BF16),
            pltpu.VMEM(weights_s.shape, BF16),
            pltpu.SemaphoreType.DMA((-(-lines_l // 64) - (-lines_s // 64),)),
        ],
        flops=2 * sum(z.lines) * 16 * LANES * LANES,
        size=2 * (weights_l.size + weights_s.size),
    )
    got = lax.all_to_all(sent, AXES, split_axis=0, concat_axis=0, tiled=True)

    small, wide = call(
        matrix_kernel,
        (models,),
        [shape((z.n_model, CHANNELS), F32), shape((z.n_model * SUB, 3 * CHANNELS * SUB), BF16)],
        16, flops=50_000_000, size=1_000_000,
    )
    rim = shape((z.n_model, LANES), F32)
    fit, rim_first, rim_last = call(
        merge_kernel,
        (got, small, wide),
        [shape((z.n_model, z.map_lines, LANES), F32), rim, rim],
        32,
        scratch=[
            pltpu.VMEM((z.devices * max(z.caps), COMPS * LANES), F32),
            pltpu.VMEM((z.devices * SUB, LANES), F32),
            pltpu.VMEM((2 * COMPS, z.map_lines, LANES), F32),
            pltpu.VMEM((z.n_model, z.map_lines + 2 * SUB, LANES), F32),
        ],
        flops=1_000_000_000,
        size=4_000_000,
    )
    above, below = exchange(rim_first, rim_last, "sec")
    ends = pl.BlockSpec((z.n_model, SUB, LANES), lambda i: (0, i * (z.map_lines // SUB - 1), 0))
    edge = pl.BlockSpec((z.n_model, LANES), lambda i: (0, 0))
    return pl.pallas_call(
        finish_kernel,
        grid=(2,),
        in_specs=[ends, edge, edge],
        out_specs=ends,
        out_shape=shape(fit.shape, F32),
        input_output_aliases={0: 0},
        compiler_params=params(16),
    )(fit, above, below)


def solution(mesh):
    in_specs = (
        P(None, "sec", "swath"),
        P(None, "sec", "swath"),
        P(("sec", "swath"), None, None),
        P(("sec", "swath"), None, None),
        P(("sec", "swath"), None),
        P(("sec", "swath"), None),
        P(("sec", "swath")),
        P(("sec", "swath")),
        P(),
    )
    out_specs = P(None, "sec", "swath")
    return jax.shard_map(body, mesh=mesh, in_specs=in_specs, out_specs=out_specs, check_vma=False)
```

profile of v0, /device:TPU:1, one launch (start us, length us, event | category | flops | bytes accessed | tf_op | source)
XLA Modules:
  0.0 108.5 jit_solution(7484319845093211637)
XLA Ops:
  0.0 0.7 reshape.13.refs_3_
  0.7 1.1 copy-done
  1.8 1.0 copy-done.2
  2.7 0.7 copy-done.4
  3.4 0.7 copy-done.5
  4.1 0.7 copy-done.6
  4.8 0.8 shard_map.91
  5.6 4.0 %collective-permute-start = (bf16[8,640]{1,0:T(8,128)(2,1)S(1)}, bf16[8,640]{1,0:T(8,128)(2,1)S(1)}, u32[]{:S(2)}, u32[]{:S(2)}) collective-permute-start(bf16[8,640]{1,0:T(8,128)(2,1)S(1)} %get-tuple-element.19), channel_id=1, source_target_pairs={{0,1},{1,2},{2,3},{3,4},{4,5},{5,6},{6,7},{8,9},{9,10},{10,11},{11... | collective-permute-start | bytes 30728 | tf_op jit(solution)/shard_map/ppermute | solution.py:48
  9.6 1.3 %collective-permute-start.1 = (bf16[8,640]{1,0:T(8,128)(2,1)S(1)}, bf16[8,640]{1,0:T(8,128)(2,1)S(1)}, u32[]{:S(2)}, u32[]{:S(2)}) collective-permute-start(bf16[8,640]{1,0:T(8,128)(2,1)S(1)} %get-tuple-element.20), channel_id=1, source_target_pairs={{1,0},{2,1},{3,2},{4,3},{5,4},{6,5},{7,6},{9,8},{10,9},{11,10},{12... | collective-permute-start | bytes 30728 | tf_op jit(solution)/shard_map/ppermute | solution.py:48
  10.9 3.1 %collective-permute-done.1.refs_5_ = bf16[8,640]{1,0:T(8,128)(2,1)S(1)} collective-permute-done((bf16[8,640]{1,0:T(8,128)(2,1)S(1)}, bf16[8,640]{1,0:T(8,128)(2,1)S(1)}, u32[]{:S(2)}, u32[]{:S(2)}) %collective-permute-start.1) | collective-permute-done | bytes 10272 | tf_op jit(solution)/shard_map/ppermute | solution.py:48
  14.0 0.1 shard_map.92
  14.1 5.1 %collective-permute-start.2 = (bf16[40,128]{1,0:T(8,128)(2,1)S(1)}, bf16[40,128]{1,0:T(8,128)(2,1)S(1)}, u32[]{:S(2)}, u32[]{:S(2)}) collective-permute-start(bf16[40,128]{1,0:T(8,128)(2,1)S(1)} %get-tuple-element.21), channel_id=1, source_target_pairs={{0,8},{8,16},{16,24},{1,9},{9,17},{17,25},{2,10},{10,18},{18,26},{... | collective-permute-start | bytes 30728 | tf_op jit(solution)/shard_map/ppermute | solution.py:48
  19.2 1.9 %collective-permute-start.3 = (bf16[40,128]{1,0:T(8,128)(2,1)S(1)}, bf16[40,128]{1,0:T(8,128)(2,1)S(1)}, u32[]{:S(2)}, u32[]{:S(2)}) collective-permute-start(bf16[40,128]{1,0:T(8,128)(2,1)S(1)} %get-tuple-element.22), channel_id=1, source_target_pairs={{8,0},{16,8},{24,16},{9,1},{17,9},{25,17},{10,2},{18,10},{26,18},{... | collective-permute-start | bytes 30728 | tf_op jit(solution)/shard_map/ppermute | solution.py:48
  21.1 3.1 %collective-permute-done.3.refs_7_ = bf16[40,128]{1,0:T(8,128)(2,1)S(1)} collective-permute-done((bf16[40,128]{1,0:T(8,128)(2,1)S(1)}, bf16[40,128]{1,0:T(8,128)(2,1)S(1)}, u32[]{:S(2)}, u32[]{:S(2)}) %collective-permute-start.3) | collective-permute-done | bytes 10272 | tf_op jit(solution)/shard_map/ppermute | solution.py:48
  24.2 12.7 %shard_map.93 = bf16[32,248,128]{2,1,0:T(8,128)(2,1)} custom-call(s32[1,384]{1,0:T(1,128)S(1)} %get-tuple-element.17.refs_0_, s32[1,256]{1,0:T(1,128)S(1)} %get-tuple-element.18.refs_1_, bf16[6,384,128]{2,1,0:T(8,128)(2,1)S(1)} %copy-done.1, bf16[6,256,128]{2,1,0:T(8,128)(2,1)S(1)} %copy-done.3, bf16[8,640]{1,0:T(8,128)(2,1)S(1)} %collective-permute-done.refs_4_, ...), custom_call_target="tpu_custom_call" | custom-call | flops 335544320 | bytes 20971520 | tf_op jit(solution)/shard_map/pallas_call | solution.py:374
  36.9 0.0 copy-start.7
  36.9 4.7 %all-to-all-start = ((bf16[32,248,128]{2,1,0:T(8,128)(2,1)}), bf16[32,248,128]{2,1,0:T(8,128)(2,1)S(1)}, u32[]{:S(2)}, u32[]{:S(2)}) async-start(bf16[32,248,128]{2,1,0:T(8,128)(2,1)} %shard_map.93), calls=%async_computation | async-start | bytes 4063232 | tf_op jit(solution)/shard_map/all_to_all | solution.py:426
  41.6 2.0 %shard_map.94 = (f32[16,36]{1,0:T(8,128)S(1)}, bf16[128,864]{1,0:T(8,128)(2,1)S(1)}) custom-call(f32[16,36]{1,0:T(8,128)S(1)} %copy-done.7), custom_call_target="tpu_custom_call" | custom-call | flops 50000000 | bytes 1000000 | tf_op jit(solution)/shard_map/pallas_call | solution.py:374
  43.6 46.0 %all-to-all-done.refs_0_ = bf16[32,248,128]{2,1,0:T(8,128)(2,1)S(1)} async-done(((bf16[32,248,128]{2,1,0:T(8,128)(2,1)}), bf16[32,248,128]{2,1,0:T(8,128)(2,1)S(1)}, u32[]{:S(2)}, u32[]{:S(2)}) %all-to-all-start) | async-done | bytes 2031648 | tf_op jit(solution)/shard_map/all_to_all | solution.py:426
  89.6 9.5 %shard_map.95 = (f32[16,256,128]{2,1,0:T(8,128)}, f32[16,128]{1,0:T(8,128)S(1)}, f32[16,128]{1,0:T(8,128)S(1)}) custom-call(bf16[32,248,128]{2,1,0:T(8,128)(2,1)S(1)} %all-to-all-done.refs_0_, f32[16,36]{1,0:T(8,128)S(1)} %get-tuple-element.24.refs_1_, bf16[128,864]{1,0:T(8,128)(2,1)S(1)} %get-tuple-element.25.refs_2_), custom_call_target="tpu_custom_call" | custom-call | flops 1000000000 | bytes 4000000 | tf_op jit(solution)/shard_map/pallas_call | solution.py:374
  99.2 2.8 %collective-permute-start.4 = (f32[16,128]{1,0:T(8,128)S(1)}, f32[16,128]{1,0:T(8,128)S(1)}, u32[]{:S(2)}, u32[]{:S(2)}) collective-permute-start(f32[16,128]{1,0:T(8,128)S(1)} %get-tuple-element.27), channel_id=1, source_target_pairs={{0,8},{8,16},{16,24},{1,9},{9,17},{17,25},{2,10},{10,18},{18,26},{... | collective-permute-start | bytes 24584 | tf_op jit(solution)/shard_map/ppermute | solution.py:48
  102.0 1.9 %collective-permute-start.5 = (f32[16,128]{1,0:T(8,128)S(1)}, f32[16,128]{1,0:T(8,128)S(1)}, u32[]{:S(2)}, u32[]{:S(2)}) collective-permute-start(f32[16,128]{1,0:T(8,128)S(1)} %get-tuple-element.28), channel_id=1, source_target_pairs={{8,0},{16,8},{24,16},{9,1},{17,9},{25,17},{10,2},{18,10},{26,18},{... | collective-permute-start | bytes 24584 | tf_op jit(solution)/shard_map/ppermute | solution.py:48
  103.9 3.0 %collective-permute-done.5.below = f32[16,128]{1,0:T(8,128)S(1)} collective-permute-done((f32[16,128]{1,0:T(8,128)S(1)}, f32[16,128]{1,0:T(8,128)S(1)}, u32[]{:S(2)}, u32[]{:S(2)}) %collective-permute-start.5) | collective-permute-done | bytes 8224 | tf_op jit(solution)/shard_map/ppermute | solution.py:48
  106.9 1.5 %shard_map.96 = f32[16,256,128]{2,1,0:T(8,128)} custom-call(f32[16,256,128]{2,1,0:T(8,128)} %get-tuple-element.26.fit, f32[16,128]{1,0:T(8,128)S(1)} %collective-permute-done.4.above, f32[16,128]{1,0:T(8,128)S(1)} %collective-permute-done.5.below), custom_call_target="tpu_custom_call", output_to_operand_aliasing={{}: (0, {})} | custom-call | tf_op jit(solution)/shard_map/pallas_call | solution.py:452
  (13 shorter events, 0.0 us)
Async XLA Ops:
  0.7 1.1 copy-start
  1.7 1.0 copy-start.2
  2.7 0.7 copy-start.4
  3.4 0.7 copy-start.5
  4.1 0.7 copy-start.6
  4.8 19.4 %copy-start.1 = (bf16[6,384,128]{2,1,0:T(8,128)(2,1)S(1)}, bf16[6,384,128]{2,1,0:T(8,128)(2,1)}, u32[]{:S(2)}) copy-start(bf16[6,384,128]{2,1,0:T(8,128)(2,1)} %refs_2_.3) | copy-start | bytes 1769476
  4.8 19.4 %copy-start.3 = (bf16[6,256,128]{2,1,0:T(8,128)(2,1)S(1)}, bf16[6,256,128]{2,1,0:T(8,128)(2,1)}, u32[]{:S(2)}) copy-start(bf16[6,256,128]{2,1,0:T(8,128)(2,1)} %refs_3_.3) | copy-start | bytes 1179652
  5.6 5.3 %collective-permute-start = (bf16[8,640]{1,0:T(8,128)(2,1)S(1)}, bf16[8,640]{1,0:T(8,128)(2,1)S(1)}, u32[]{:S(2)}, u32[]{:S(2)}) collective-permute-start(bf16[8,640]{1,0:T(8,128)(2,1)S(1)} %get-tuple-element.19), channel_id=1, source_target_pairs={{0,1},{1,2},{2,3},{3,4},{4,5},{5,6},{6,7},{8,9},{9,10},{10,11},{11... | collective-permute-start | bytes 30728 | tf_op jit(solution)/shard_map/ppermute | solution.py:48
  9.6 4.4 %collective-permute-start.1 = (bf16[8,640]{1,0:T(8,128)(2,1)S(1)}, bf16[8,640]{1,0:T(8,128)(2,1)S(1)}, u32[]{:S(2)}, u32[]{:S(2)}) collective-permute-start(bf16[8,640]{1,0:T(8,128)(2,1)S(1)} %get-tuple-element.20), channel_id=1, source_target_pairs={{1,0},{2,1},{3,2},{4,3},{5,4},{6,5},{7,6},{9,8},{10,9},{11,10},{12... | collective-permute-start | bytes 30728 | tf_op jit(solution)/shard_map/ppermute | solution.py:48
  14.1 7.0 %collective-permute-start.2 = (bf16[40,128]{1,0:T(8,128)(2,1)S(1)}, bf16[40,128]{1,0:T(8,128)(2,1)S(1)}, u32[]{:S(2)}, u32[]{:S(2)}) collective-permute-start(bf16[40,128]{1,0:T(8,128)(2,1)S(1)} %get-tuple-element.21), channel_id=1, source_target_pairs={{0,8},{8,16},{16,24},{1,9},{9,17},{17,25},{2,10},{10,18},{18,26},{... | collective-permute-start | bytes 30728 | tf_op jit(solution)/shard_map/ppermute | solution.py:48
  19.2 5.0 %collective-permute-start.3 = (bf16[40,128]{1,0:T(8,128)(2,1)S(1)}, bf16[40,128]{1,0:T(8,128)(2,1)S(1)}, u32[]{:S(2)}, u32[]{:S(2)}) collective-permute-start(bf16[40,128]{1,0:T(8,128)(2,1)S(1)} %get-tuple-element.22), channel_id=1, source_target_pairs={{8,0},{16,8},{24,16},{9,1},{17,9},{25,17},{10,2},{18,10},{26,18},{... | collective-permute-start | bytes 30728 | tf_op jit(solution)/shard_map/ppermute | solution.py:48
  36.9 4.7 %copy-start.7 = (f32[16,36]{1,0:T(8,128)S(1)}, f32[16,36]{1,0:T(8,128)}, u32[]{:S(2)}) copy-start(f32[16,36]{1,0:T(8,128)} %refs_0_.5) | copy-start | bytes 6916
  36.9 52.7 %all-to-all-start = ((bf16[32,248,128]{2,1,0:T(8,128)(2,1)}), bf16[32,248,128]{2,1,0:T(8,128)(2,1)S(1)}, u32[]{:S(2)}, u32[]{:S(2)}) async-start(bf16[32,248,128]{2,1,0:T(8,128)(2,1)} %shard_map.93), calls=%async_computation | async-start | bytes 4063232 | tf_op jit(solution)/shard_map/all_to_all | solution.py:426
  99.2 4.7 %collective-permute-start.4 = (f32[16,128]{1,0:T(8,128)S(1)}, f32[16,128]{1,0:T(8,128)S(1)}, u32[]{:S(2)}, u32[]{:S(2)}) collective-permute-start(f32[16,128]{1,0:T(8,128)S(1)} %get-tuple-element.27), channel_id=1, source_target_pairs={{0,8},{8,16},{16,24},{1,9},{9,17},{17,25},{2,10},{10,18},{18,26},{... | collective-permute-start | bytes 24584 | tf_op jit(solution)/shard_map/ppermute | solution.py:48
  102.0 5.0 %collective-permute-start.5 = (f32[16,128]{1,0:T(8,128)S(1)}, f32[16,128]{1,0:T(8,128)S(1)}, u32[]{:S(2)}, u32[]{:S(2)}) collective-permute-start(f32[16,128]{1,0:T(8,128)S(1)} %get-tuple-element.28), channel_id=1, source_target_pairs={{8,0},{16,8},{24,16},{9,1},{17,9},{25,17},{10,2},{18,10},{26,18},{... | collective-permute-start | bytes 24584 | tf_op jit(solution)/shard_map/ppermute | solution.py:48
where the time goes:
time: 109 us; the launch traced here: 108 us
  waiting for transfers between devices  55.2 us (51%)
  Pallas kernels  26.6 us (24%)
  starting transfers between devices  21.7 us (20%)
  local copies, waits for them, and re-layouts  4.79 us (4%)
    all_to_all x1, waiting for transfers between devices, body(): got = lax.all_to_all(sent, AXES, split_axis=0, concat_axis=0, tiled=True)  46 us
    pallas_call x4, Pallas kernels, call(): pl.pallas_call(lambda *refs: kernel(z, *refs) if kernel is not matrix_ker...  25.1 us
    ppermute x6, starting transfers between devices, exchange(): return (lax.ppermute(last, axis, up), lax.ppermute(first, axis, down))  17 us
    ppermute x6, waiting for transfers between devices, exchange(): return (lax.ppermute(last, axis, up), lax.ppermute(first, axis, down))  9.2 us
    all_to_all x1, starting transfers between devices, body(): got = lax.all_to_all(sent, AXES, split_axis=0, concat_axis=0, tiled=True)  4.68 us
    unnamed x16, local copies, waits for them, and re-layouts  4.11 us
  transfers between devices with their start and end apart: 7, of which 4 were waited for; matrix products, arithmetic and copies ran while one was open for 0% of the time, Pallas kernels for 2%

commit v1 on v0

--- a/solution.py
+++ b/solution.py
@@ -50,6 +50,11 @@
 
 VMEM = pl.BlockSpec(memory_space=pltpu.VMEM)
 SMEM = pl.BlockSpec(memory_space=pltpu.SMEM)
+ANY = pl.BlockSpec(memory_space=pl.ANY)
+
+
+def whole(shape):
+    return pl.BlockSpec(shape, lambda i: (0,) * len(shape))
 
 
 def up_to(n, multiple):
@@ -68,23 +73,23 @@
         self.rows = up_to(COMPS * sum(self.caps), SUB)
         self.stride = up_to(self.rows + SUB, LANES)
         self.lanes = up_to(self.rows, LANES)
-
-
-def first_kernel(z, radar_l, radar_s, owner_l, slot_l, owner_s, slot_s, first, last, base_l, base_s, marks):
-    wide = COMPS * LANES
-    pick = iota((2 * SUB, wide), 1) == jnp.where(
-        iota((2 * SUB, wide), 0) < SUB,
-        iota((2 * SUB, wide), 0) * LANES,
-        (iota((2 * SUB, wide), 0) - SUB) * LANES + LANES - 1,
-    )
-    pick = ones_where(pick)
-    at = 0
+        self.part = 64 if lines_l % 64 == 0 and map_lines % 64 == 0 else 2
+
+
+def first_kernel(z, radar_l, radar_s, first, last):
+    shape = (2 * SUB, COMPS * LANES)
+    row, at = iota(shape, 0), iota(shape, 1)
+    pick = ones_where(at == jnp.where(row < SUB, row * LANES, (row - SUB) * LANES + LANES - 1))
+    start = 0
     for radar, lines in ((radar_l, z.lines[0]), (radar_s, z.lines[1])):
         rows = jnp.concatenate([radar[c] for c in range(COMPS)], axis=1)
         both = dot(pick, rows, NT)
-        first[:, at : at + lines] = both[0:SUB].astype(BF16)
-        last[:, at : at + lines] = both[SUB:].astype(BF16)
-        at += lines
+        first[:, start : start + lines] = both[0:SUB].astype(BF16)
+        last[:, start : start + lines] = both[SUB:].astype(BF16)
+        start += lines
+
+
+def plan_kernel(z, owner_l, slot_l, owner_s, slot_s, base_l, base_s, marks):
     total = jnp.zeros((z.devices, LANES), F32)
     shift = 0
     for band, (owner, slot, base) in enumerate(((owner_l, slot_l, base_l), (owner_s, slot_s, base_s))):
@@ -99,11 +104,10 @@
         total = total + dot(line, place, NT)
         shift += z.caps[band]
     me, other = iota((z.devices, z.devices), 0), iota((z.devices, z.devices), 1)
-    swath = z.swath
-    inner = iota((z.devices, z.devices), 0) % swath
+    inner = me % z.swath
     own = total.astype(BF16)
     before = dot(ones_where((other == me - 1) & (inner > 0)), own, NN)
-    after = dot(ones_where((other == me + 1) & (inner < swath - 1)), own, NN)
+    after = dot(ones_where((other == me + 1) & (inner < z.swath - 1)), own, NN)
     marks[...] = total + pltpu.roll(before, shift, 1) + pltpu.roll(after, 2 * shift, 1)
 
 
@@ -132,97 +136,132 @@
     return before, after
 
 
-def filter_band(band, tiles, radar, left, right, above, below, work, filtered):
+def filter_band(tiles, radar, left, right, work, filtered):
     inner = pl.ds(SUB, tiles)
-    ends = ((SUB - 1, above), (SUB + tiles, below))
-
-    def end_values(strip, c):
-        row = band * COMPS + c
-        corner = 2 * COMPS + row
-        return strip[row : row + 1], strip[corner : corner + 1, 0:1], strip[corner + 2 * COMPS : corner + 2 * COMPS + 1, 0:1]
-
-    def power_of(values):
-        total = [0.0, 0.0, 0.0]
-        for triple in values:
-            total = [t + v * v for t, v in zip(total, triple)]
-        return (total[0],) + with_sides(*total)
-
+    blank = jnp.zeros((1, LANES), F32)
+    for plane in range(3):
+        work[plane, SUB - 1 : SUB, :] = blank
+        work[plane, SUB + tiles : SUB + tiles + 1, :] = blank
     body = [radar[c].astype(F32) for c in range(COMPS)]
     lefts = [left[:, c : c + 1] for c in range(COMPS)]
     rights = [right[:, c : c + 1] for c in range(COMPS)]
-    for plane, value in enumerate(power_of(zip(body, lefts, rights))):
+    squares = lambda values: sum(v * v for v in values)
+    power = squares(body)
+    for plane, value in enumerate((power,) + with_sides(power, squares(lefts), squares(rights))):
         work[plane, inner, :] = value
-    for row, strip in ends:
-        for plane, value in enumerate(power_of([end_values(strip, c) for c in range(COMPS)])):
-            work[plane, pl.ds(row, 1), :] = value
     near = [work[plane, pl.ds(SUB + d, tiles), :] for plane in range(3) for d in (-1, 0, 1)]
+    gain = gain_of(near)
+    for c in range(COMPS):
+        plane = c % 3
+        before, after = with_sides(body[c], lefts[c], rights[c])
+        work[plane, inner, :] = body[c] + before + after
+        mean = work[plane, pl.ds(SUB - 1, tiles), :] + work[plane, inner, :]
+        mean = (mean + work[plane, pl.ds(SUB + 1, tiles), :]) / 9.0
+        filtered[pl.ds(c, tiles, stride=SUB), :] = mean + gain * (body[c] - mean)
+
+
+def gain_of(near):
     mean_power = sum(near[1:], near[0]) / 9.0
     spread = jnp.zeros_like(mean_power)
     for q in near:
         spread = spread + (q - mean_power) ** 2
     spread = spread / 9.0
-    gain = spread / (spread + cu_square * mean_power * mean_power + 1.0)
-    for c in range(COMPS):
-        plane = c % 3
-        before, after = with_sides(body[c], lefts[c], rights[c])
-        work[plane, inner, :] = body[c] + before + after
-        for row, strip in ends:
-            x, corner_left, corner_right = end_values(strip, c)
-            before, after = with_sides(x, corner_left, corner_right)
-            work[plane, pl.ds(row, 1), :] = x + before + after
-        mean = work[plane, pl.ds(SUB - 1, tiles), :] + work[plane, inner, :]
-        mean = (mean + work[plane, pl.ds(SUB + 1, tiles), :]) / 9.0
-        filtered[pl.ds(c, tiles, stride=SUB), :] = mean + gain * (body[c] - mean)
+    return spread / (spread + cu_square * mean_power * mean_power + 1.0)
 
 
 def send_kernel(
-    z, base_l, base_s, radar_l, radar_s, before, after, above, below, marks, weights_l, weights_s,
-    out, work, filtered, packed, held_l, held_s, arrived,
+    z, base_l, base_s, radar_l, radar_s, before, after, weights_l, weights_s,
+    packed, edge_lines, edge_tiles, work, filtered, held_l, held_s, arrived,
 ):
-    chunks = []
+    chunks, count = [], 0
     for source, held, lines in ((weights_l, held_l, z.lines[0]), (weights_s, held_s, z.lines[1])):
-        size = 64 if lines % 64 == 0 else lines
         copies = []
-        for at in range(0, lines, size):
-            part = pl.ds(at, size)
-            copies.append(
-                pltpu.make_async_copy(source.at[part], held.at[part], arrived.at[sum(map(len, chunks)) + len(copies)])
-            )
+        for at in range(0, lines, z.part):
+            part = pl.ds(at, z.part)
+            copies.append(pltpu.make_async_copy(source.at[part], held.at[part], arrived.at[count]))
             copies[-1].start()
+            count += 1
         chunks.append(copies)
     packed[...] = jnp.zeros_like(packed)
+    tall = edge_lines.shape[3]
+    for band, radar in enumerate((radar_l, radar_s)):
+        edge_lines[band, 0] = radar[:, 0:tall, :]
+        edge_lines[band, 1] = radar[:, z.lines[band] - tall :, :]
     left, right = before[...].astype(F32).T, after[...].astype(F32).T
-    up, down = above[...].astype(F32), below[...].astype(F32)
     at = 0
-    for band, (radar, base, weights) in enumerate(
-        ((radar_l, base_l, held_l), (radar_s, base_s, held_s))
-    ):
+    for band, (radar, base, held) in enumerate(((radar_l, base_l, held_l), (radar_s, base_s, held_s))):
         tiles, capacity = z.lines[band], z.caps[band]
-        filter_band(
-            band, tiles, radar, left[at : at + tiles], right[at : at + tiles], up, down, work, filtered
-        )
+        filter_band(tiles, radar, left[at : at + tiles], right[at : at + tiles], work, filtered)
         at += tiles
-
-        size = tiles // len(chunks[band])
         for i, copy in enumerate(chunks[band]):
             copy.wait()
-            for t in range(0, size, 2):
-                tile = i * size + t
+            for t in range(0, z.part, 2):
+                tile = i * z.part + t
                 lines = filtered[pl.ds(tile * SUB, 2 * SUB), :].astype(BF16)
-                matrix = weights[pl.ds(tile, 2)].reshape(2 * LANES, LANES)
+                matrix = held[pl.ds(tile, 2)].reshape(2 * LANES, LANES)
                 result = dot(lines, matrix, NT)
                 first, second = base[0, tile], base[0, tile + 1]
                 packed[pl.ds(first, COMPS, stride=capacity), :] = result[0:COMPS, 0:LANES]
                 packed[pl.ds(second, COMPS, stride=capacity), :] = result[SUB : SUB + COMPS, LANES:]
+        edge_tiles[band, 0] = held[0]
+        edge_tiles[band, 1] = held[tiles - 1]
+
+
+def tail_kernel(
+    z, base_l, base_s, given, above, below, before, after, marks,
+    lines_held, tiles_held, out, packed,
+):
+    del given
+    tall = lines_held.shape[3]
+    up, down = above[...].astype(F32), below[...].astype(F32)
+    shift = 0
+    for band, base in enumerate((base_l, base_s)):
+        lines = z.lines[band]
+        for end in range(2):
+            rows = lines_held[band, end].astype(F32)
+            strip = (up, down)[end]
+            first = 0 if end == 0 else lines - 2
+            near_row = 0 if end == 0 else tall - 2
+            tile = (shift + first) // LANES * LANES
+            columns = [side[:, tile : tile + LANES].astype(F32) for side in (before, after)]
+            values, sides = [], [[], []]
+            for c in range(COMPS):
+                row = band * COMPS + c
+                far = strip[row : row + 1]
+                near = rows[c, near_row : near_row + 2]
+                values.append(jnp.concatenate([far, near] if end == 0 else [near, far], axis=0))
+                for side in range(2):
+                    corner = 2 * COMPS * (1 + side) + row
+                    far = strip[corner : corner + 1, 0:1]
+                    near = [
+                        columns[side][c : c + 1, shift + first - tile + k : shift + first - tile + k + 1]
+                        for k in range(2)
+                    ]
+                    sides[side].append(jnp.concatenate([far] + near if end == 0 else near + [far], axis=0))
+            squares = lambda parts: sum(v * v for v in parts)
+            power = squares(values)
+            planes = (power,) + with_sides(power, squares(sides[0]), squares(sides[1]))
+            gain = gain_of([plane[k : k + 1] for plane in planes for k in range(3)])
+            lines_out = []
+            for c in range(COMPS):
+                left, right = with_sides(values[c], sides[0][c], sides[1][c])
+                total = values[c] + left + right
+                mean = (total[0:1] + total[1:2] + total[2:3]) / 9.0
+                lines_out.append(mean + gain * (values[c][1:2] - mean))
+            lines_out.append(jnp.zeros((SUB - COMPS, LANES), F32))
+            result = dot(jnp.concatenate(lines_out, axis=0).astype(BF16), tiles_held[band, end], NT)
+            target = base[0, 0 if end == 0 else lines - 1]
+            packed[pl.ds(target, COMPS, stride=z.caps[band]), :] = result[0:COMPS]
+        shift += lines
 
     steps = z.lanes // LANES
     row, lane = iota((SUB, LANES), 0), iota((SUB, LANES), 1)
     pick = ones_where(
         ((row >= 1) & (row <= steps) & (lane == LANES - 1)) | ((row > steps) & (row <= 2 * steps) & (lane == 0))
     )
-    columns = []
-    for o in range(z.devices):
-        columns.append(dot(pick, packed[o * z.stride : o * z.stride + z.lanes, :].astype(BF16), NT))
+    columns = [
+        dot(pick, packed[o * z.stride : o * z.stride + z.lanes, :].astype(BF16), NT) for o in range(z.devices)
+    ]
     for o in range(z.devices):
         extra = jnp.broadcast_to(marks[o : o + 1, :], (SUB, LANES))
         one_less, one_more = max(o - 1, 0), min(o + 1, z.devices - 1)
@@ -230,9 +269,8 @@
             part = slice(k * LANES, (k + 1) * LANES)
             extra = jnp.where(row == 1 + k, columns[one_less][:, part], extra)
             extra = jnp.where(row == 1 + steps + k, columns[one_more][:, part], extra)
-        packed[o * z.stride + z.rows : o * z.stride + z.rows + SUB, :] = extra
-    for o in range(z.devices):
-        out[o] = packed[o * z.stride : o * z.stride + z.rows + SUB, :].astype(BF16)
+        out[o, 0 : z.rows, :] = packed[o * z.stride : o * z.stride + z.rows, :].astype(BF16)
+        out[o, z.rows :, :] = extra.astype(BF16)
 
 
 def matrix_kernel(models, small, wide):
@@ -245,7 +283,7 @@
         powers = powers + fit_rate * dot(m, eye - predicted, NN, HI)
     powers = powers / 9.0
     small[...] = powers
-    rows, columns = wide.shape[0], wide.shape[1] // 3
+    rows, columns = wide.shape[0] // 2, wide.shape[1]
     left = ones_where(iota((rows, n_model), 0) // SUB == iota((rows, n_model), 1), F32)
     right = ones_where(iota((CHANNELS, columns), 1) // SUB == iota((CHANNELS, columns), 0), F32)
     spread = dot(dot(left, powers, NN, HI), right, NN, HI)
@@ -253,7 +291,7 @@
     spread = jnp.where(same, spread, 0.0)
     high = spread.astype(BF16)
     low = (spread - high.astype(F32)).astype(BF16)
-    wide[...] = jnp.concatenate([high, high, low], axis=1)
+    wide[...] = jnp.concatenate([high, low], axis=0)
 
 
 def coherency(real, imag):
@@ -318,7 +356,14 @@
     turned = []
     for side in range(2):
         joint = jnp.concatenate(coherency(*split_parts(lambda i: edges[side][i])), axis=0)
-        turned.append(dot(small[...], joint, NN, HI).T)
+        turned.append(dot(small[...], joint, NN, HI))
+    x = jnp.concatenate(turned, axis=0)
+    high = x.astype(BF16)
+    x = jnp.concatenate([high, (x - high.astype(F32)).astype(BF16)], axis=0)
+    at = iota((4 * n_model, n_model * LANES), 0) % (2 * n_model)
+    to = iota((4 * n_model, n_model * LANES), 1)
+    target = jnp.where(at < n_model, at * LANES + LANES - 1, (at - n_model) * LANES)
+    planes = dot(x, ones_where(to == target), TN)
 
     matrix = wide[...]
 
@@ -327,11 +372,9 @@
         for h in range(2):
             r = pl.multiple_of((2 * i + h) * SUB, SUB)
             x = jnp.concatenate(coherency(*split_parts(lambda n: maps[n, pl.ds(r, SUB), :])), axis=0)
-            halves.append(x)
-        x = jnp.concatenate(halves, axis=1)
-        high = x.astype(BF16)
-        low = (x - high.astype(F32)).astype(BF16)
-        result = dot(matrix, jnp.concatenate([high, low, high], axis=0), NN)
+            halves.append(x.astype(BF16))
+        result = dot(matrix, jnp.concatenate(halves, axis=1), NN)
+        result = result[0 : n_model * SUB] + result[n_model * SUB :]
         for h in range(2):
             r = pl.multiple_of((2 * i + h) * SUB, SUB)
             for k in range(n_model):
@@ -340,12 +383,15 @@
                 ]
         return _
 
-    lax.fori_loop(0, map_lines // (2 * SUB), step, 0)
+    lax.fori_loop(0, map_lines // (2 * SUB), step, 0, unroll=True)
     blank = jnp.zeros((1, LANES), F32)
     inner = pl.ds(SUB, map_lines)
     for k in range(n_model):
         x = fits[k, inner, :]
-        before, after = with_sides(x, turned[0][:, k : k + 1], turned[1][:, k : k + 1])
+        side = planes[:, k * LANES : (k + 1) * LANES]
+        lane = iota(x.shape, 1)
+        before = pltpu.roll(jnp.where(lane == LANES - 1, side, x), 1, 1)
+        after = pltpu.roll(jnp.where(lane == 0, side, x), LANES - 1, 1)
         x = x + before + after
         fits[k, inner, :] = x
         fits[k, SUB - 1 : SUB, :] = blank
@@ -381,54 +427,84 @@
             cost_estimate=pl.CostEstimate(flops=flops, bytes_accessed=size, transcendentals=0),
         )(*args)
 
+    def call_one(kernel, args, specs, shapes, mib, scratch=(), aliases={}, flops=0, size=0):
+        return pl.pallas_call(
+            lambda *refs: kernel(z, *refs),
+            grid=(1,),
+            in_specs=specs,
+            out_specs=[whole(x.shape) for x in shapes],
+            out_shape=shapes,
+            scratch_shapes=scratch,
+            input_output_aliases=aliases,
+            compiler_params=params(mib),
+            cost_estimate=pl.CostEstimate(flops=flops, bytes_accessed=size, transcendentals=0),
+        )(*args)
+
     row = lambda x: x.reshape(1, -1)
+    radar = (radar_l, radar_s)
     column = shape((SUB, lines_l + lines_s), BF16)
-    first, last, base_l, base_s, marks = call(
-        first_kernel,
-        (radar_l, radar_s, row(owner_l), row(slot_l), row(owner_s), row(slot_s)),
-        [column, column, shape((1, lines_l), jnp.int32), shape((1, lines_s), jnp.int32), shape((z.devices, LANES), F32)],
-        16, flops=30_000_000, size=2_000_000,
+    first, last = call_one(
+        first_kernel, radar, [whole(x.shape) for x in radar], [column, column], 60,
+        flops=10_000_000, size=1_000_000,
     )
     before, after = exchange(first, last, "swath")
+    owners = (row(owner_l), row(slot_l), row(owner_s), row(slot_s))
+    base_l, base_s, marks = call_one(
+        plan_kernel,
+        owners,
+        [whole(x.shape) for x in owners],
+        [shape((1, lines_l), jnp.int32), shape((1, lines_s), jnp.int32), shape((z.devices, LANES), F32)],
+        16, flops=1_000_000_000, size=1_000_000,
+    )
     strip = shape((5 * SUB, LANES), BF16)
     tall = 2 * SUB
     edge = lambda lines, end: pl.BlockSpec(
         (COMPS, tall, LANES), lambda i: (0, end * (lines // tall - 1), 0)
     )
-    side = pl.BlockSpec(before.shape, lambda i: (0, 0))
-    first, last = pl.pallas_call(
-        lambda *refs: second_kernel(z, *refs),
-        grid=(1,),
-        in_specs=[edge(lines, end) for end in range(2) for lines in z.lines] + [side, side],
-        out_specs=[pl.BlockSpec(strip.shape, lambda i: (0, 0))] * 2,
-        out_shape=[strip, strip],
-        compiler_params=params(16),
-    )(radar_l, radar_s, radar_l, radar_s, before, after)
+    edges = [edge(lines, end) for end in range(2) for lines in z.lines]
+    side = whole(column.shape)
+    first, last = call_one(
+        second_kernel, radar * 2 + (before, after), edges + [side, side], [strip, strip], 32,
+    )
     above, below = exchange(first, last, "sec")
-    args = (base_l, base_s, radar_l, radar_s, before, after, above, below, marks, weights_l, weights_s)
-    (sent,) = call(
+    smem = lambda x: pl.BlockSpec(x.shape, lambda i: (0, 0), memory_space=pltpu.SMEM)
+    bases = [smem(base_l), smem(base_s)]
+    buffer = shape((z.devices * z.stride + up_to(COMPS * max(z.caps), SUB), LANES), F32)
+    packed, edge_lines, edge_tiles = call(
         send_kernel,
-        args,
-        [shape((z.devices, z.rows + SUB, LANES), BF16)],
+        (base_l, base_s, radar_l, radar_s, before, after, weights_l, weights_s),
+        [
+            buffer,
+            shape((2, 2, COMPS, tall, LANES), BF16),
+            shape((2, 2, LANES, LANES), BF16),
+        ],
         44,
-        specs=[SMEM, SMEM] + [VMEM] * (len(args) - 4) + [pl.BlockSpec(memory_space=pl.ANY)] * 2,
+        specs=[SMEM, SMEM] + [VMEM] * 4 + [ANY] * 2,
         scratch=[
             pltpu.VMEM((3, max(z.lines) + 2 * SUB, LANES), F32),
             pltpu.VMEM((max(z.lines) * SUB, LANES), F32),
-            pltpu.VMEM((z.devices * z.stride + up_to(COMPS * max(z.caps), SUB), LANES), F32),
             pltpu.VMEM(weights_l.shape, BF16),
             pltpu.VMEM(weights_s.shape, BF16),
-            pltpu.SemaphoreType.DMA((-(-lines_l // 64) - (-lines_s // 64),)),
+            pltpu.SemaphoreType.DMA((sum(z.lines) // z.part,)),
         ],
-        flops=2 * sum(z.lines) * 16 * LANES * LANES,
+        flops=10_000_000_000,
         size=2 * (weights_l.size + weights_s.size),
     )
+    args = (base_l, base_s, packed, above, below, before, after, marks, edge_lines, edge_tiles)
+    sent, _ = pl.pallas_call(
+        lambda *refs: tail_kernel(z, *refs),
+        in_specs=[SMEM, SMEM] + [VMEM] * 8,
+        out_specs=[VMEM, VMEM],
+        out_shape=[shape((z.devices, z.rows + SUB, LANES), BF16), buffer],
+        input_output_aliases={2: 1},
+        compiler_params=params(24),
+    )(*args)
     got = lax.all_to_all(sent, AXES, split_axis=0, concat_axis=0, tiled=True)
 
     small, wide = call(
         matrix_kernel,
         (models,),
-        [shape((z.n_model, CHANNELS), F32), shape((z.n_model * SUB, 3 * CHANNELS * SUB), BF16)],
+        [shape((z.n_model, CHANNELS), F32), shape((2 * z.n_model * SUB, CHANNELS * SUB), BF16)],
         16, flops=50_000_000, size=1_000_000,
     )
     rim = shape((z.n_model, LANES), F32)

time: 109 us -> 101 us (0.927)
  waiting for transfers between devices: 55.2 us -> 49.2 us
  local copies, waits for them, and re-layouts: 4.79 us -> 2.74 us
  Pallas kernels: 26.6 us -> 25 us
  starting transfers between devices: 21.7 us -> 23.2 us
    pallas_call x4 -> x3, Pallas kernels: 25.1 us -> 17.6 us  [call(): pl.pallas_call(lambda *refs: kernel(z, *refs) if kernel is not matrix_ker...]
    ppermute x6, waiting for transfers between devices: 9.2 us -> 3.06 us  [exchange(): return (lax.ppermute(last, axis, up), lax.ppermute(first, axis, down))]
    pallas_call x1 -> x4, Pallas kernels: 0.08 us -> 5.85 us  [the longest x1 2.96 us: body(): pl.pallas_call(lambda *refs: tail_kernel(z, *refs), in_specs=[SMEM, SMEM]...]
    unnamed x16 -> x12, local copies, waits for them, and re-layouts: 4.11 us -> 2.05 us
    all_to_all x1, starting transfers between devices: 4.68 us -> 6.22 us  [body(): got = lax.all_to_all(sent, AXES, split_axis=0, concat_axis=0, tiled=True)]
  transfers between devices with their start and end apart: 7 -> 7, of which waited for: 4 -> 2; matrix products, arithmetic and copies ran while one was open for 0% -> 1% of each run, Pallas kernels for 2% -> 13%
where the time goes in v1:
time: 101 us; the launch traced here: 100 us
  waiting for transfers between devices  49.2 us (49%)
  Pallas kernels  25 us (25%)
  starting transfers between devices  23.2 us (23%)
  local copies, waits for them, and re-layouts  2.74 us (3%)
    all_to_all x1, waiting for transfers between devices, body(): got = lax.all_to_all(sent, AXES, split_axis=0, concat_axis=0, tiled=True)  46.1 us
    pallas_call x3, Pallas kernels, call(): pl.pallas_call(lambda *refs: kernel(z, *refs) if kernel is not matrix_ker...  17.6 us
    ppermute x6, starting transfers between devices, exchange(): return (lax.ppermute(last, axis, up), lax.ppermute(first, axis, down))  17 us
    all_to_all x1, starting transfers between devices, body(): got = lax.all_to_all(sent, AXES, split_axis=0, concat_axis=0, tiled=True)  6.22 us
    ppermute x6, waiting for transfers between devices, exchange(): return (lax.ppermute(last, axis, up), lax.ppermute(first, axis, down))  3.06 us
    pallas_call x1, Pallas kernels, body(): pl.pallas_call(lambda *refs: tail_kernel(z, *refs), in_specs=[SMEM, SMEM]...  2.96 us
    pallas_call x3, Pallas kernels, call_one(): pl.pallas_call(lambda *refs: kernel(z, *refs), grid=(1,), in_specs=specs,...  2.9 us
    unnamed x12, local copies, waits for them, and re-layouts  2.05 us
  transfers between devices with their start and end apart: 7, of which 2 were waited for; matrix products, arithmetic and copies ran while one was open for 1% of the time, Pallas kernels for 13%

profile of v1, /device:TPU:1, one launch (start us, length us, event | category | flops | bytes accessed | tf_op | source)
XLA Modules:
  0.0 100.2 jit_solution(648453102863163979)
XLA Ops:
  0.0 2.2 %shard_map.92 = (bf16[8,640]{1,0:T(8,128)(2,1)}, bf16[8,640]{1,0:T(8,128)(2,1)}) custom-call(bf16[6,384,128]{2,1,0:T(8,128)(2,1)} %refs_2_.3, bf16[6,256,128]{2,1,0:T(8,128)(2,1)} %refs_3_.3), custom_call_target="tpu_custom_call" | custom-call | flops 10000000 | bytes 1000000 | tf_op jit(solution)/shard_map/pallas_call | solution.py:431
  2.3 3.9 %collective-permute-start = (bf16[8,640]{1,0:T(8,128)(2,1)}, bf16[8,640]{1,0:T(8,128)(2,1)S(1)}, u32[]{:S(2)}, u32[]{:S(2)}) collective-permute-start(bf16[8,640]{1,0:T(8,128)(2,1)} %get-tuple-element.23), channel_id=1, source_target_pairs={{0,1},{1,2},{2,3},{3,4},{4,5},{5,6},{6,7},{8,9},{9,10},{10,11},{11... | collective-permute-start | bytes 30728 | tf_op jit(solution)/shard_map/ppermute | solution.py:48
  6.2 1.3 %collective-permute-start.1 = (bf16[8,640]{1,0:T(8,128)(2,1)}, bf16[8,640]{1,0:T(8,128)(2,1)S(1)}, u32[]{:S(2)}, u32[]{:S(2)}) collective-permute-start(bf16[8,640]{1,0:T(8,128)(2,1)} %get-tuple-element.24), channel_id=1, source_target_pairs={{1,0},{2,1},{3,2},{4,3},{5,4},{6,5},{7,6},{9,8},{10,9},{11,10},{12... | collective-permute-start | bytes 30728 | tf_op jit(solution)/shard_map/ppermute | solution.py:48
  7.5 0.7 reshape.13.refs_1_
  8.2 0.7 copy-done.3
  8.9 0.7 copy-done.4
  9.6 0.7 copy-done.5
  10.2 0.6 shard_map.91
  10.8 0.0 collective-permute-done.refs_4_.refs_5_
  10.8 0.0 collective-permute-done.1.refs_5_.refs_6_
  10.9 0.1 shard_map.94
  10.9 5.1 %collective-permute-start.2 = (bf16[40,128]{1,0:T(8,128)(2,1)S(1)}, bf16[40,128]{1,0:T(8,128)(2,1)S(1)}, u32[]{:S(2)}, u32[]{:S(2)}) collective-permute-start(bf16[40,128]{1,0:T(8,128)(2,1)S(1)} %get-tuple-element.26), channel_id=1, source_target_pairs={{0,8},{8,16},{16,24},{1,9},{9,17},{17,25},{2,10},{10,18},{18,26},{... | collective-permute-start | bytes 30728 | tf_op jit(solution)/shard_map/ppermute | solution.py:48
  16.0 1.9 %collective-permute-start.3 = (bf16[40,128]{1,0:T(8,128)(2,1)S(1)}, bf16[40,128]{1,0:T(8,128)(2,1)S(1)}, u32[]{:S(2)}, u32[]{:S(2)}) collective-permute-start(bf16[40,128]{1,0:T(8,128)(2,1)S(1)} %get-tuple-element.27), channel_id=1, source_target_pairs={{8,0},{16,8},{24,16},{9,1},{17,9},{25,17},{10,2},{18,10},{26,18},{... | collective-permute-start | bytes 30728 | tf_op jit(solution)/shard_map/ppermute | solution.py:48
  18.0 10.6 %shard_map.93 = (f32[8336,128]{1,0:T(8,128)S(1)}, bf16[2,2,6,16,128]{4,3,2,1,0:T(8,128)(2,1)S(1)}, bf16[2,2,128,128]{3,2,1,0:T(8,128)(2,1)S(1)}) custom-call(s32[1,384]{1,0:T(1,128)S(1)} %get-tuple-element.21.refs_0_, s32[1,256]{1,0:T(1,128)S(1)} %get-tuple-element.22.refs_1_, bf16[6,384,128]{2,1,0:T(8,128)(2,1)S(1)} %copy-done, ...), custom_call_target="tpu_custom_call" | custom-call | flops 10000000000 | bytes 20971520 | tf_op jit(solution)/shard_map/pallas_call | solution.py:420
  28.6 0.0 copy-start.2
  28.6 3.0 %shard_map.95 = (bf16[32,248,128]{2,1,0:T(8,128)(2,1)}, f32[8336,128]{1,0:T(8,128)S(1)}) custom-call(s32[1,384]{1,0:T(1,128)S(1)} %get-tuple-element.21.refs_0_, s32[1,256]{1,0:T(1,128)S(1)} %get-tuple-element.22.refs_1_, f32[8336,128]{1,0:T(8,128)S(1)} %get-tuple-element.25.refs_2_, ...), custom_call_target="tpu_custom_call", output_to_operand_aliasing={{1}: (2, {})} | custom-call | tf_op jit(solution)/shard_map/pallas_call | solution.py:494
  31.5 6.2 %all-to-all-start = ((bf16[32,248,128]{2,1,0:T(8,128)(2,1)}), bf16[32,248,128]{2,1,0:T(8,128)(2,1)S(1)}, u32[]{:S(2)}, u32[]{:S(2)}) async-start(bf16[32,248,128]{2,1,0:T(8,128)(2,1)} %get-tuple-element.31), calls=%async_computation | async-start | bytes 4063232 | tf_op jit(solution)/shard_map/all_to_all | solution.py:502
  37.8 1.9 %shard_map.96 = (f32[16,36]{1,0:T(8,128)S(1)}, bf16[256,288]{1,0:T(8,128)(2,1)S(1)}) custom-call(f32[16,36]{1,0:T(8,128)S(1)} %copy-done.2), custom_call_target="tpu_custom_call" | custom-call | flops 50000000 | bytes 1000000 | tf_op jit(solution)/shard_map/pallas_call | solution.py:420
  39.7 46.1 %all-to-all-done.refs_0_ = bf16[32,248,128]{2,1,0:T(8,128)(2,1)S(1)} async-done(((bf16[32,248,128]{2,1,0:T(8,128)(2,1)}), bf16[32,248,128]{2,1,0:T(8,128)(2,1)S(1)}, u32[]{:S(2)}, u32[]{:S(2)}) %all-to-all-start) | async-done | bytes 2031648 | tf_op jit(solution)/shard_map/all_to_all | solution.py:502
  85.8 5.1 %shard_map.97 = (f32[16,256,128]{2,1,0:T(8,128)}, f32[16,128]{1,0:T(8,128)S(1)}, f32[16,128]{1,0:T(8,128)S(1)}) custom-call(bf16[32,248,128]{2,1,0:T(8,128)(2,1)S(1)} %all-to-all-done.refs_0_, f32[16,36]{1,0:T(8,128)S(1)} %get-tuple-element.32.refs_1_, bf16[256,288]{1,0:T(8,128)(2,1)S(1)} %get-tuple-element.33.refs_2_), custom_call_target="tpu_custom_call" | custom-call | flops 1000000000 | bytes 4000000 | tf_op jit(solution)/shard_map/pallas_call | solution.py:420
  90.9 2.8 %collective-permute-start.4 = (f32[16,128]{1,0:T(8,128)S(1)}, f32[16,128]{1,0:T(8,128)S(1)}, u32[]{:S(2)}, u32[]{:S(2)}) collective-permute-start(f32[16,128]{1,0:T(8,128)S(1)} %get-tuple-element.35), channel_id=1, source_target_pairs={{0,8},{8,16},{16,24},{1,9},{9,17},{17,25},{2,10},{10,18},{18,26},{... | collective-permute-start | bytes 24584 | tf_op jit(solution)/shard_map/ppermute | solution.py:48
  93.7 1.9 %collective-permute-start.5 = (f32[16,128]{1,0:T(8,128)S(1)}, f32[16,128]{1,0:T(8,128)S(1)}, u32[]{:S(2)}, u32[]{:S(2)}) collective-permute-start(f32[16,128]{1,0:T(8,128)S(1)} %get-tuple-element.36), channel_id=1, source_target_pairs={{8,0},{16,8},{24,16},{9,1},{17,9},{25,17},{10,2},{18,10},{26,18},{... | collective-permute-start | bytes 24584 | tf_op jit(solution)/shard_map/ppermute | solution.py:48
  95.7 3.0 %collective-permute-done.5.below = f32[16,128]{1,0:T(8,128)S(1)} collective-permute-done((f32[16,128]{1,0:T(8,128)S(1)}, f32[16,128]{1,0:T(8,128)S(1)}, u32[]{:S(2)}, u32[]{:S(2)}) %collective-permute-start.5) | collective-permute-done | bytes 8224 | tf_op jit(solution)/shard_map/ppermute | solution.py:48
  98.7 1.5 %shard_map.98 = f32[16,256,128]{2,1,0:T(8,128)} custom-call(f32[16,256,128]{2,1,0:T(8,128)} %get-tuple-element.34.fit, f32[16,128]{1,0:T(8,128)S(1)} %collective-permute-done.4.above, f32[16,128]{1,0:T(8,128)S(1)} %collective-permute-done.5.below), custom_call_target="tpu_custom_call", output_to_operand_aliasing={{}: (0, {})} | custom-call | tf_op jit(solution)/shard_map/pallas_call | solution.py:528
  (11 shorter events, 0.0 us)
Async XLA Ops:
  0.0 10.8 %copy-start.1 = (bf16[6,256,128]{2,1,0:T(8,128)(2,1)S(1)}, bf16[6,256,128]{2,1,0:T(8,128)(2,1)}, u32[]{:S(2)}) copy-start(bf16[6,256,128]{2,1,0:T(8,128)(2,1)} %refs_3_.3) | copy-start | bytes 1179652
  0.0 10.8 %copy-start = (bf16[6,384,128]{2,1,0:T(8,128)(2,1)S(1)}, bf16[6,384,128]{2,1,0:T(8,128)(2,1)}, u32[]{:S(2)}) copy-start(bf16[6,384,128]{2,1,0:T(8,128)(2,1)} %refs_2_.3) | copy-start | bytes 1769476
  2.3 8.6 %collective-permute-start = (bf16[8,640]{1,0:T(8,128)(2,1)}, bf16[8,640]{1,0:T(8,128)(2,1)S(1)}, u32[]{:S(2)}, u32[]{:S(2)}) collective-permute-start(bf16[8,640]{1,0:T(8,128)(2,1)} %get-tuple-element.23), channel_id=1, source_target_pairs={{0,1},{1,2},{2,3},{3,4},{4,5},{5,6},{6,7},{8,9},{9,10},{10,11},{11... | collective-permute-start | bytes 30728 | tf_op jit(solution)/shard_map/ppermute | solution.py:48
  6.2 4.6 %collective-permute-start.1 = (bf16[8,640]{1,0:T(8,128)(2,1)}, bf16[8,640]{1,0:T(8,128)(2,1)S(1)}, u32[]{:S(2)}, u32[]{:S(2)}) collective-permute-start(bf16[8,640]{1,0:T(8,128)(2,1)} %get-tuple-element.24), channel_id=1, source_target_pairs={{1,0},{2,1},{3,2},{4,3},{5,4},{6,5},{7,6},{9,8},{10,9},{11,10},{12... | collective-permute-start | bytes 30728 | tf_op jit(solution)/shard_map/ppermute | solution.py:48
  8.2 0.7 copy-start.3
  8.9 0.7 copy-start.4
  9.6 0.7 copy-start.5
  10.9 17.6 %collective-permute-start.2 = (bf16[40,128]{1,0:T(8,128)(2,1)S(1)}, bf16[40,128]{1,0:T(8,128)(2,1)S(1)}, u32[]{:S(2)}, u32[]{:S(2)}) collective-permute-start(bf16[40,128]{1,0:T(8,128)(2,1)S(1)} %get-tuple-element.26), channel_id=1, source_target_pairs={{0,8},{8,16},{16,24},{1,9},{9,17},{17,25},{2,10},{10,18},{18,26},{... | collective-permute-start | bytes 30728 | tf_op jit(solution)/shard_map/ppermute | solution.py:48
  16.0 12.5 %collective-permute-start.3 = (bf16[40,128]{1,0:T(8,128)(2,1)S(1)}, bf16[40,128]{1,0:T(8,128)(2,1)S(1)}, u32[]{:S(2)}, u32[]{:S(2)}) collective-permute-start(bf16[40,128]{1,0:T(8,128)(2,1)S(1)} %get-tuple-element.27), channel_id=1, source_target_pairs={{8,0},{16,8},{24,16},{9,1},{17,9},{25,17},{10,2},{18,10},{26,18},{... | collective-permute-start | bytes 30728 | tf_op jit(solution)/shard_map/ppermute | solution.py:48
  28.6 9.2 %copy-start.2 = (f32[16,36]{1,0:T(8,128)S(1)}, f32[16,36]{1,0:T(8,128)}, u32[]{:S(2)}) copy-start(f32[16,36]{1,0:T(8,128)} %refs_0_.5) | copy-start | bytes 6916
  31.5 54.3 %all-to-all-start = ((bf16[32,248,128]{2,1,0:T(8,128)(2,1)}), bf16[32,248,128]{2,1,0:T(8,128)(2,1)S(1)}, u32[]{:S(2)}, u32[]{:S(2)}) async-start(bf16[32,248,128]{2,1,0:T(8,128)(2,1)} %get-tuple-element.31), calls=%async_computation | async-start | bytes 4063232 | tf_op jit(solution)/shard_map/all_to_all | solution.py:502
  90.9 4.7 %collective-permute-start.4 = (f32[16,128]{1,0:T(8,128)S(1)}, f32[16,128]{1,0:T(8,128)S(1)}, u32[]{:S(2)}, u32[]{:S(2)}) collective-permute-start(f32[16,128]{1,0:T(8,128)S(1)} %get-tuple-element.35), channel_id=1, source_target_pairs={{0,8},{8,16},{16,24},{1,9},{9,17},{17,25},{2,10},{10,18},{18,26},{... | collective-permute-start | bytes 24584 | tf_op jit(solution)/shard_map/ppermute | solution.py:48
  93.7 5.0 %collective-permute-start.5 = (f32[16,128]{1,0:T(8,128)S(1)}, f32[16,128]{1,0:T(8,128)S(1)}, u32[]{:S(2)}, u32[]{:S(2)}) collective-permute-start(f32[16,128]{1,0:T(8,128)S(1)} %get-tuple-element.36), channel_id=1, source_target_pairs={{8,0},{16,8},{24,16},{9,1},{17,9},{25,17},{10,2},{18,10},{26,18},{... | collective-permute-start | bytes 24584 | tf_op jit(solution)/shard_map/ppermute | solution.py:48

commit v2 on v1

--- a/solution.py
+++ b/solution.py
@@ -41,11 +41,15 @@
     return jnp.where(mask, 1.0, 0.0).astype(dtype)
 
 
-def exchange(first, last, axis):
+def swap(even_pairs, odd_pairs, axis):
     peers = lax.axis_size(axis)
-    up = [(i, i + 1) for i in range(peers - 1)]
-    down = [(j, i) for i, j in up]
-    return lax.ppermute(last, axis, up), lax.ppermute(first, axis, down)
+    pairs = lambda start: [p for i in range(start, peers - 1, 2) for p in ((i, i + 1), (i + 1, i))]
+    return lax.ppermute(even_pairs, axis, pairs(0)), lax.ppermute(odd_pairs, axis, pairs(1))
+
+
+def by_parity(axis, one, other):
+    even = lax.axis_index(axis) % 2 == 0
+    return jnp.where(even, one, other), jnp.where(even, other, one)
 
 
 VMEM = pl.BlockSpec(memory_space=pltpu.VMEM)
@@ -76,7 +80,10 @@
         self.part = 64 if lines_l % 64 == 0 and map_lines % 64 == 0 else 2
 
 
-def first_kernel(z, radar_l, radar_s, first, last):
+def first_kernel(
+    z, radar_l, radar_s, owner_l, slot_l, owner_s, slot_s, even_pairs, odd_pairs, base_l, base_s, marks
+):
+    plan(z, owner_l, slot_l, owner_s, slot_s, base_l, base_s, marks)
     shape = (2 * SUB, COMPS * LANES)
     row, at = iota(shape, 0), iota(shape, 1)
     pick = ones_where(at == jnp.where(row < SUB, row * LANES, (row - SUB) * LANES + LANES - 1))
@@ -84,12 +91,13 @@
     for radar, lines in ((radar_l, z.lines[0]), (radar_s, z.lines[1])):
         rows = jnp.concatenate([radar[c] for c in range(COMPS)], axis=1)
         both = dot(pick, rows, NT)
-        first[:, start : start + lines] = both[0:SUB].astype(BF16)
-        last[:, start : start + lines] = both[SUB:].astype(BF16)
+        one, other = by_parity("swath", both[SUB:], both[0:SUB])
+        even_pairs[:, start : start + lines] = one.astype(BF16)
+        odd_pairs[:, start : start + lines] = other.astype(BF16)
         start += lines
 
 
-def plan_kernel(z, owner_l, slot_l, owner_s, slot_s, base_l, base_s, marks):
+def plan(z, owner_l, slot_l, owner_s, slot_s, base_l, base_s, marks):
     total = jnp.zeros((z.devices, LANES), F32)
     shift = 0
     for band, (owner, slot, base) in enumerate(((owner_l, slot_l, base_l), (owner_s, slot_s, base_s))):
@@ -99,7 +107,7 @@
         before = dot(ones_where(hit), earlier, NN)
         rank = jnp.sum(jnp.where(hit, before, 0.0), axis=0, keepdims=True).astype(jnp.int32)
         base[...] = owner[...] * z.stride + z.starts[band] + rank
-        line = jnp.where(hit, slot[...] + 1, 0).astype(F32).astype(BF16)
+        line = jnp.where(hit, slot[...].reshape(1, tiles) + 1, 0).astype(F32).astype(BF16)
         place = ones_where(iota((LANES, tiles), 0) == rank + shift)
         total = total + dot(line, place, NT)
         shift += z.caps[band]
@@ -111,21 +119,25 @@
     marks[...] = total + pltpu.roll(before, shift, 1) + pltpu.roll(after, 2 * shift, 1)
 
 
-def second_kernel(z, top_l, top_s, bottom_l, bottom_s, before, after, first, last):
+def second_kernel(z, top_l, top_s, bottom_l, bottom_s, swap_a, swap_b, even_pairs, odd_pairs):
+    after, before = by_parity("swath", swap_a[...].astype(F32), swap_b[...].astype(F32))
+    strips = []
     lines_l, lines_s = z.lines
     ends = (
-        (first, top_l, top_s, 0, 0, lines_l),
-        (last, bottom_l, bottom_s, top_l.shape[1] - 1, lines_l - 1, lines_l + lines_s - 1),
-    )
-    for out, rows_l, rows_s, row, at_l, at_s in ends:
+        (top_l, top_s, 0, 0, lines_l),
+        (bottom_l, bottom_s, top_l.shape[1] - 1, lines_l - 1, lines_l + lines_s - 1),
+    )
+    for rows_l, rows_s, row, at_l, at_s in ends:
         parts = [rows_l[...].astype(F32)[:, row, :], rows_s[...].astype(F32)[:, row, :]]
         for side in (before, after):
             for at in (at_l, at_s):
-                tile = at // LANES * LANES
-                column = side[:, tile : tile + LANES].astype(F32)[0:COMPS, at - tile : at - tile + 1]
+                column = side[0:COMPS, at : at + 1]
                 parts.append(jnp.broadcast_to(column, (COMPS, LANES)))
-        parts.append(jnp.zeros((out.shape[0] - 6 * COMPS, LANES), F32))
-        out[...] = jnp.concatenate(parts, axis=0).astype(BF16)
+        parts.append(jnp.zeros((even_pairs.shape[0] - 6 * COMPS, LANES), F32))
+        strips.append(jnp.concatenate(parts, axis=0))
+    one, other = by_parity("sec", strips[1], strips[0])
+    even_pairs[...] = one.astype(BF16)
+    odd_pairs[...] = other.astype(BF16)
 
 
 def with_sides(x, left, right):
@@ -170,7 +182,7 @@
 
 
 def send_kernel(
-    z, base_l, base_s, radar_l, radar_s, before, after, weights_l, weights_s,
+    z, base_l, base_s, radar_l, radar_s, swap_a, swap_b, weights_l, weights_s,
     packed, edge_lines, edge_tiles, work, filtered, held_l, held_s, arrived,
 ):
     chunks, count = [], 0
@@ -187,7 +199,8 @@
     for band, radar in enumerate((radar_l, radar_s)):
         edge_lines[band, 0] = radar[:, 0:tall, :]
         edge_lines[band, 1] = radar[:, z.lines[band] - tall :, :]
-    left, right = before[...].astype(F32).T, after[...].astype(F32).T
+    after, before = by_parity("swath", swap_a[...].astype(F32), swap_b[...].astype(F32))
+    left, right = before.T, after.T
     at = 0
     for band, (radar, base, held) in enumerate(((radar_l, base_l, held_l), (radar_s, base_s, held_s))):
         tiles, capacity = z.lines[band], z.caps[band]
@@ -208,12 +221,13 @@
 
 
 def tail_kernel(
-    z, base_l, base_s, given, above, below, before, after, marks,
+    z, base_l, base_s, given, sec_a, sec_b, swap_a, swap_b, marks,
     lines_held, tiles_held, out, packed,
 ):
     del given
     tall = lines_held.shape[3]
-    up, down = above[...].astype(F32), below[...].astype(F32)
+    after, before = by_parity("swath", swap_a[...].astype(F32), swap_b[...].astype(F32))
+    down, up = by_parity("sec", sec_a[...].astype(F32), sec_b[...].astype(F32))
     shift = 0
     for band, base in enumerate((base_l, base_s)):
         lines = z.lines[band]
@@ -222,8 +236,7 @@
             strip = (up, down)[end]
             first = 0 if end == 0 else lines - 2
             near_row = 0 if end == 0 else tall - 2
-            tile = (shift + first) // LANES * LANES
-            columns = [side[:, tile : tile + LANES].astype(F32) for side in (before, after)]
+            columns = (before, after)
             values, sides = [], [[], []]
             for c in range(COMPS):
                 row = band * COMPS + c
@@ -234,7 +247,7 @@
                     corner = 2 * COMPS * (1 + side) + row
                     far = strip[corner : corner + 1, 0:1]
                     near = [
-                        columns[side][c : c + 1, shift + first - tile + k : shift + first - tile + k + 1]
+                        columns[side][c : c + 1, shift + first + k : shift + first + k + 1]
                         for k in range(2)
                     ]
                     sides[side].append(jnp.concatenate([far] + near if end == 0 else near + [far], axis=0))
@@ -304,7 +317,7 @@
     return pick(0), pick(3)
 
 
-def merge_kernel(z, got, small, wide, out, rim_first, rim_last, stage, extras, maps, fits):
+def merge_kernel(z, got, small, wide, out, even_pairs, odd_pairs, stage, extras, maps, fits):
     map_lines, n_model, devices = z.map_lines, z.n_model, z.devices
     steps = z.lanes // LANES
     for s in range(devices):
@@ -396,19 +409,28 @@
         fits[k, inner, :] = x
         fits[k, SUB - 1 : SUB, :] = blank
         fits[k, SUB + map_lines : SUB + map_lines + 1, :] = blank
-        rim_first[k : k + 1, :] = x[0:1, :]
-        rim_last[k : k + 1, :] = x[map_lines - 1 :, :]
+        one, other = by_parity("sec", x[map_lines - 1 :, :], x[0:1, :])
+        even_pairs[k : k + 1, :] = one
+        odd_pairs[k : k + 1, :] = other
         out[k] = fits[k, pl.ds(SUB - 1, map_lines), :] + x + fits[k, pl.ds(SUB + 1, map_lines), :]
 
 
-def finish_kernel(fit, above, below, out):
-    end = pl.program_id(0)
-    line = iota(fit.shape[1:], 0)
-    height = fit.shape[1]
-    for k in range(fit.shape[0]):
-        upper = jnp.where((line == 0) & (end == 0), above[k : k + 1, :], 0.0)
-        lower = jnp.where((line == height - 1) & (end == 1), below[k : k + 1, :], 0.0)
-        out[k] = fit[k] + upper + lower
+def finish_kernel(z, given, sec_a, sec_b, out, ends, moving):
+    parts = (pl.ds(0, SUB), pl.ds(z.map_lines - SUB, SUB))
+    copies = [pltpu.make_async_copy(given.at[:, p, :], ends.at[k], moving.at[k]) for k, p in enumerate(parts)]
+    for copy in copies:
+        copy.start()
+    below, above = by_parity("sec", sec_a[...], sec_b[...])
+    line = iota((SUB, LANES), 0)
+    for copy in copies:
+        copy.wait()
+    copies = [pltpu.make_async_copy(ends.at[k], out.at[:, p, :], moving.at[2 + k]) for k, p in enumerate(parts)]
+    for end, (at, row) in enumerate(((0, above), (SUB - 1, below))):
+        for k in range(z.n_model):
+            ends[end, k] = ends[end, k] + jnp.where(line == at, row[k : k + 1, :], 0.0)
+        copies[end].start()
+    for copy in copies:
+        copy.wait()
 
 
 def body(radar_l, radar_s, weights_l, weights_s, owner_l, owner_s, slot_l, slot_s, models):
@@ -443,19 +465,17 @@
     row = lambda x: x.reshape(1, -1)
     radar = (radar_l, radar_s)
     column = shape((SUB, lines_l + lines_s), BF16)
-    first, last = call_one(
-        first_kernel, radar, [whole(x.shape) for x in radar], [column, column], 60,
-        flops=10_000_000, size=1_000_000,
-    )
-    before, after = exchange(first, last, "swath")
-    owners = (row(owner_l), row(slot_l), row(owner_s), row(slot_s))
-    base_l, base_s, marks = call_one(
-        plan_kernel,
-        owners,
-        [whole(x.shape) for x in owners],
-        [shape((1, lines_l), jnp.int32), shape((1, lines_s), jnp.int32), shape((z.devices, LANES), F32)],
-        16, flops=1_000_000_000, size=1_000_000,
-    )
+    args = radar + (row(owner_l), slot_l, row(owner_s), slot_s)
+    even, odd, base_l, base_s, marks = call_one(
+        first_kernel,
+        args,
+        [whole(x.shape) for x in args],
+        [column, column, shape((1, lines_l), jnp.int32), shape((1, lines_s), jnp.int32), shape((z.devices, LANES), F32)],
+        58,
+        flops=10_000_000_000,
+        size=1_000_000,
+    )
+    swap_a, swap_b = swap(even, odd, "swath")
     strip = shape((5 * SUB, LANES), BF16)
     tall = 2 * SUB
     edge = lambda lines, end: pl.BlockSpec(
@@ -463,16 +483,14 @@
     )
     edges = [edge(lines, end) for end in range(2) for lines in z.lines]
     side = whole(column.shape)
-    first, last = call_one(
-        second_kernel, radar * 2 + (before, after), edges + [side, side], [strip, strip], 32,
-    )
-    above, below = exchange(first, last, "sec")
-    smem = lambda x: pl.BlockSpec(x.shape, lambda i: (0, 0), memory_space=pltpu.SMEM)
-    bases = [smem(base_l), smem(base_s)]
+    even, odd = call_one(
+        second_kernel, radar * 2 + (swap_a, swap_b), edges + [side, side], [strip, strip], 32, flops=10_000_000_000, size=1_000_000,
+    )
+    sec_a, sec_b = swap(even, odd, "sec")
     buffer = shape((z.devices * z.stride + up_to(COMPS * max(z.caps), SUB), LANES), F32)
     packed, edge_lines, edge_tiles = call(
         send_kernel,
-        (base_l, base_s, radar_l, radar_s, before, after, weights_l, weights_s),
+        (base_l, base_s, radar_l, radar_s, swap_a, swap_b, weights_l, weights_s),
         [
             buffer,
             shape((2, 2, COMPS, tall, LANES), BF16),
@@ -490,7 +508,7 @@
         flops=10_000_000_000,
         size=2 * (weights_l.size + weights_s.size),
     )
-    args = (base_l, base_s, packed, above, below, before, after, marks, edge_lines, edge_tiles)
+    args = (base_l, base_s, packed, sec_a, sec_b, swap_a, swap_b, marks, edge_lines, edge_tiles)
     sent, _ = pl.pallas_call(
         lambda *refs: tail_kernel(z, *refs),
         in_specs=[SMEM, SMEM] + [VMEM] * 8,
@@ -508,7 +526,7 @@
         16, flops=50_000_000, size=1_000_000,
     )
     rim = shape((z.n_model, LANES), F32)
-    fit, rim_first, rim_last = call(
+    fit, even, odd = call(
         merge_kernel,
         (got, small, wide),
         [shape((z.n_model, z.map_lines, LANES), F32), rim, rim],
@@ -522,18 +540,16 @@
         flops=1_000_000_000,
         size=4_000_000,
     )
-    above, below = exchange(rim_first, rim_last, "sec")
-    ends = pl.BlockSpec((z.n_model, SUB, LANES), lambda i: (0, i * (z.map_lines // SUB - 1), 0))
-    edge = pl.BlockSpec((z.n_model, LANES), lambda i: (0, 0))
+    sec_a, sec_b = swap(even, odd, "sec")
     return pl.pallas_call(
-        finish_kernel,
-        grid=(2,),
-        in_specs=[ends, edge, edge],
-        out_specs=ends,
+        lambda *refs: finish_kernel(z, *refs),
+        in_specs=[ANY, VMEM, VMEM],
+        out_specs=ANY,
         out_shape=shape(fit.shape, F32),
+        scratch_shapes=[pltpu.VMEM((2, z.n_model, SUB, LANES), F32), pltpu.SemaphoreType.DMA((4,))],
         input_output_aliases={0: 0},
         compiler_params=params(16),
-    )(fit, above, below)
+    )(fit, sec_a, sec_b)
 
 
 def solution(mesh):

time: 101 us -> 94.4 us (0.935)
  starting transfers between devices: 23.2 us -> 19.7 us
  local copies, waits for them, and re-layouts: 2.74 us -> 0.03 us
    ppermute x6, starting transfers between devices: 17 us -> 11.1 us  [the longest x3 6.64 us: swap(): lax.ppermute(odd_pairs, axis, pairs(1))]
    all_to_all x1, starting transfers between devices: 6.22 us -> 8.6 us  [body(): got = lax.all_to_all(sent, AXES, split_axis=0, concat_axis=0, tiled=True)]
    unnamed x12, local copies, waits for them, and re-layouts: 2.05 us -> 0.03 us
    pallas_call x3 -> x2, Pallas kernels: 2.9 us -> 2.76 us  [call_one(): pl.pallas_call(lambda *refs: kernel(z, *refs), grid=(1,), in_specs=specs,...]
  transfers between devices with their start and end apart: 7 -> 7, of which waited for: 2 -> 3; matrix products, arithmetic and copies ran while one was open for 1% -> 0% of each run, Pallas kernels for 13% -> 13%
where the time goes in v2:
time: 94.4 us; the launch traced here: 94.1 us
  waiting for transfers between devices  49.2 us (52%)
  Pallas kernels  24.9 us (26%)
  starting transfers between devices  19.7 us (21%)
    all_to_all x1, waiting for transfers between devices, body(): got = lax.all_to_all(sent, AXES, split_axis=0, concat_axis=0, tiled=True)  46.1 us
    pallas_call x3, Pallas kernels, call(): pl.pallas_call(lambda *refs: kernel(z, *refs) if kernel is not matrix_ker...  17.6 us
    all_to_all x1, starting transfers between devices, body(): got = lax.all_to_all(sent, AXES, split_axis=0, concat_axis=0, tiled=True)  8.6 us
    ppermute x3, starting transfers between devices, swap(): lax.ppermute(odd_pairs, axis, pairs(1))  6.64 us
    ppermute x3, starting transfers between devices, swap(): lax.ppermute(even_pairs, axis, pairs(0))  4.47 us
    pallas_call x1, Pallas kernels, body(): pl.pallas_call(lambda *refs: tail_kernel(z, *refs), in_specs=[SMEM, SMEM]...  2.98 us
    pallas_call x2, Pallas kernels, call_one(): pl.pallas_call(lambda *refs: kernel(z, *refs), grid=(1,), in_specs=specs,...  2.76 us
    ppermute x3, waiting for transfers between devices, swap(): lax.ppermute(odd_pairs, axis, pairs(1))  2.61 us
  transfers between devices with their start and end apart: 7, of which 3 were waited for; matrix products, arithmetic and copies ran while one was open for 0% of the time, Pallas kernels for 13%

profile of v2, /device:TPU:1, one launch (start us, length us, event | category | flops | bytes accessed | tf_op | source)
XLA Modules:
  0.0 94.1 jit_solution(10811939086003867117)
XLA Ops:
  0.0 2.7 %shard_map.91 = (bf16[8,640]{1,0:T(8,128)(2,1)}, bf16[8,640]{1,0:T(8,128)(2,1)}, s32[1,384]{1,0:T(1,128)}, s32[1,256]{1,0:T(1,128)}, f32[32,128]{1,0:T(8,128)}) custom-call(bf16[6,384,128]{2,1,0:T(8,128)(2,1)} %refs_2_.3, bf16[6,256,128]{2,1,0:T(8,128)(2,1)} %refs_3_.5, s32[1,384]{1,0:T(1,128)} %bitcast.2, s32[384]{0:T(512)} %refs_3_.3, s32[1,256]{1,0:T(1,128)} %bitcast.3, ...), custom_call_target="tpu_custom_call" | custom-call | flops 10000000000 | bytes 1000000 | tf_op jit(solution)/shard_map/pallas_call | solution.py:453
  2.7 2.1 %collective-permute-start = (bf16[8,640]{1,0:T(8,128)(2,1)}, bf16[8,640]{1,0:T(8,128)(2,1)S(1)}, u32[]{:S(2)}, u32[]{:S(2)}) collective-permute-start(bf16[8,640]{1,0:T(8,128)(2,1)} %get-tuple-element.23), channel_id=1, source_target_pairs={{0,1},{1,0},{2,3},{3,2},{4,5},{5,4},{6,7},{7,6},{8,9},{9,8},{10,11... | collective-permute-start | bytes 30728 | tf_op jit(solution)/shard_map/ppermute | solution.py:47
  4.7 0.8 collective-permute-start.1
  5.5 0.5 collective-permute-done.refs_4_.refs_5_
  6.0 0.0 collective-permute-done.1.refs_5_.refs_6_
  6.0 0.1 shard_map.93
  6.1 1.6 %collective-permute-start.2 = (bf16[40,128]{1,0:T(8,128)(2,1)S(1)}, bf16[40,128]{1,0:T(8,128)(2,1)S(1)}, u32[]{:S(2)}, u32[]{:S(2)}) collective-permute-start(bf16[40,128]{1,0:T(8,128)(2,1)S(1)} %get-tuple-element.26), channel_id=1, source_target_pairs={{0,8},{8,0},{16,24},{24,16},{1,9},{9,1},{17,25},{25,17},{2,10},{10... | collective-permute-start | bytes 30728 | tf_op jit(solution)/shard_map/ppermute | solution.py:47
  7.7 3.5 %collective-permute-start.3 = (bf16[40,128]{1,0:T(8,128)(2,1)S(1)}, bf16[40,128]{1,0:T(8,128)(2,1)S(1)}, u32[]{:S(2)}, u32[]{:S(2)}) collective-permute-start(bf16[40,128]{1,0:T(8,128)(2,1)S(1)} %get-tuple-element.27), channel_id=1, source_target_pairs={{8,16},{16,8},{9,17},{17,9},{10,18},{18,10},{11,19},{19,11},{12,20... | collective-permute-start | bytes 30728 | tf_op jit(solution)/shard_map/ppermute | solution.py:47
  11.2 0.0 copy-start
  11.2 10.6 %shard_map.92 = (f32[8336,128]{1,0:T(8,128)S(1)}, bf16[2,2,6,16,128]{4,3,2,1,0:T(8,128)(2,1)S(1)}, bf16[2,2,128,128]{3,2,1,0:T(8,128)(2,1)S(1)}) custom-call(s32[1,384]{1,0:T(1,128)S(1)} %copy-done.1, s32[1,256]{1,0:T(1,128)S(1)} %copy-done.2, bf16[6,384,128]{2,1,0:T(8,128)(2,1)S(1)} %copy-done.3, bf16[6,256,128]{2,1,0:T(8,128)(2,1)S(1)} %copy-done.4, ...), custom_call_target="tpu_custom_call" | custom-call | flops 10000000000 | bytes 20971520 | tf_op jit(solution)/shard_map/pallas_call | solution.py:442
  21.8 0.0 collective-permute-done.2.refs_3_
  21.8 0.0 collective-permute-done.3.refs_4_
  21.8 0.0 copy-start.5
  21.8 3.0 %shard_map.94 = (bf16[32,248,128]{2,1,0:T(8,128)(2,1)}, f32[8336,128]{1,0:T(8,128)S(1)}) custom-call(s32[1,384]{1,0:T(1,128)S(1)} %copy-done.1, s32[1,256]{1,0:T(1,128)S(1)} %copy-done.2, f32[8336,128]{1,0:T(8,128)S(1)} %get-tuple-element.25.refs_2_, bf16[40,128]{1,0:T(8,128)(2,1)S(1)} %collective-permute-done.2.refs_3_, ...), custom_call_target="tpu_custom_call", output_to_operand_aliasing={{1}: (2, {})} | custom-call | tf_op jit(solution)/shard_map/pallas_call | solution.py:512
  24.8 8.6 %all-to-all-start = ((bf16[32,248,128]{2,1,0:T(8,128)(2,1)}), bf16[32,248,128]{2,1,0:T(8,128)(2,1)S(1)}, u32[]{:S(2)}, u32[]{:S(2)}) async-start(bf16[32,248,128]{2,1,0:T(8,128)(2,1)} %get-tuple-element.31), calls=%async_computation | async-start | bytes 4063232 | tf_op jit(solution)/shard_map/all_to_all | solution.py:520
  33.4 0.0 copy-done.5
  33.4 1.9 %shard_map.95 = (f32[16,36]{1,0:T(8,128)S(1)}, bf16[256,288]{1,0:T(8,128)(2,1)S(1)}) custom-call(f32[16,36]{1,0:T(8,128)S(1)} %copy-done.5), custom_call_target="tpu_custom_call" | custom-call | flops 50000000 | bytes 1000000 | tf_op jit(solution)/shard_map/pallas_call | solution.py:442
  35.4 46.1 %all-to-all-done.refs_0_ = bf16[32,248,128]{2,1,0:T(8,128)(2,1)S(1)} async-done(((bf16[32,248,128]{2,1,0:T(8,128)(2,1)}), bf16[32,248,128]{2,1,0:T(8,128)(2,1)S(1)}, u32[]{:S(2)}, u32[]{:S(2)}) %all-to-all-start) | async-done | bytes 2031648 | tf_op jit(solution)/shard_map/all_to_all | solution.py:520
  81.5 5.1 %shard_map.96 = (f32[16,256,128]{2,1,0:T(8,128)}, f32[16,128]{1,0:T(8,128)S(1)}, f32[16,128]{1,0:T(8,128)S(1)}) custom-call(bf16[32,248,128]{2,1,0:T(8,128)(2,1)S(1)} %all-to-all-done.refs_0_, f32[16,36]{1,0:T(8,128)S(1)} %get-tuple-element.32.refs_1_, bf16[256,288]{1,0:T(8,128)(2,1)S(1)} %get-tuple-element.33.refs_2_), custom_call_target="tpu_custom_call" | custom-call | flops 1000000000 | bytes 4000000 | tf_op jit(solution)/shard_map/pallas_call | solution.py:442
  86.6 0.9 collective-permute-start.4
  87.4 2.3 %collective-permute-start.5 = (f32[16,128]{1,0:T(8,128)S(1)}, f32[16,128]{1,0:T(8,128)S(1)}, u32[]{:S(2)}, u32[]{:S(2)}) collective-permute-start(f32[16,128]{1,0:T(8,128)S(1)} %get-tuple-element.36), channel_id=1, source_target_pairs={{8,16},{16,8},{9,17},{17,9},{10,18},{18,10},{11,19},{19,11},{12,20... | collective-permute-start | bytes 24584 | tf_op jit(solution)/shard_map/ppermute | solution.py:47
  89.8 0.0 collective-permute-done.4.refs_1_
  89.8 2.6 %collective-permute-done.5.refs_2_ = f32[16,128]{1,0:T(8,128)S(1)} collective-permute-done((f32[16,128]{1,0:T(8,128)S(1)}, f32[16,128]{1,0:T(8,128)S(1)}, u32[]{:S(2)}, u32[]{:S(2)}) %collective-permute-start.5) | collective-permute-done | bytes 8224 | tf_op jit(solution)/shard_map/ppermute | solution.py:47
  92.4 1.6 %shard_map.97 = f32[16,256,128]{2,1,0:T(8,128)} custom-call(f32[16,256,128]{2,1,0:T(8,128)} %get-tuple-element.34.refs_0_, f32[16,128]{1,0:T(8,128)S(1)} %collective-permute-done.4.refs_1_, f32[16,128]{1,0:T(8,128)S(1)} %collective-permute-done.5.refs_2_), custom_call_target="tpu_custom_call", output_to_operand_aliasing={{}: (0, {})} | custom-call | tf_op jit(solution)/shard_map/pallas_call | solution.py:544
  (9 shorter events, 0.0 us)
Async XLA Ops:
  0.0 6.0 %copy-start.3 = (bf16[6,384,128]{2,1,0:T(8,128)(2,1)S(1)}, bf16[6,384,128]{2,1,0:T(8,128)(2,1)}, u32[]{:S(2)}) copy-start(bf16[6,384,128]{2,1,0:T(8,128)(2,1)} %refs_2_.3) | copy-start | bytes 1769476
  0.0 6.0 %copy-start.4 = (bf16[6,256,128]{2,1,0:T(8,128)(2,1)S(1)}, bf16[6,256,128]{2,1,0:T(8,128)(2,1)}, u32[]{:S(2)}) copy-start(bf16[6,256,128]{2,1,0:T(8,128)(2,1)} %refs_3_.5) | copy-start | bytes 1179652
  2.7 3.3 %collective-permute-start = (bf16[8,640]{1,0:T(8,128)(2,1)}, bf16[8,640]{1,0:T(8,128)(2,1)S(1)}, u32[]{:S(2)}, u32[]{:S(2)}) collective-permute-start(bf16[8,640]{1,0:T(8,128)(2,1)} %get-tuple-element.23), channel_id=1, source_target_pairs={{0,1},{1,0},{2,3},{3,2},{4,5},{5,4},{6,7},{7,6},{8,9},{9,8},{10,11... | collective-permute-start | bytes 30728 | tf_op jit(solution)/shard_map/ppermute | solution.py:47
  4.7 6.5 %copy-start.1 = (s32[1,384]{1,0:T(1,128)S(1)}, s32[1,384]{1,0:T(1,128)}, u32[]{:S(2)}) copy-start(s32[1,384]{1,0:T(1,128)} %get-tuple-element.21.refs_0_) | copy-start | bytes 4612
  4.7 6.5 %copy-start.2 = (s32[1,256]{1,0:T(1,128)S(1)}, s32[1,256]{1,0:T(1,128)}, u32[]{:S(2)}) copy-start(s32[1,256]{1,0:T(1,128)} %get-tuple-element.22.refs_1_) | copy-start | bytes 3076
  4.7 1.3 %collective-permute-start.1 = (bf16[8,640]{1,0:T(8,128)(2,1)}, bf16[8,640]{1,0:T(8,128)(2,1)S(1)}, u32[]{:S(2)}, u32[]{:S(2)}) collective-permute-start(bf16[8,640]{1,0:T(8,128)(2,1)} %get-tuple-element.24), channel_id=1, source_target_pairs={{1,2},{2,1},{3,4},{4,3},{5,6},{6,5},{9,10},{10,9},{11,12},{12,11},... | collective-permute-start | bytes 30728 | tf_op jit(solution)/shard_map/ppermute | solution.py:47
  6.1 15.7 %collective-permute-start.2 = (bf16[40,128]{1,0:T(8,128)(2,1)S(1)}, bf16[40,128]{1,0:T(8,128)(2,1)S(1)}, u32[]{:S(2)}, u32[]{:S(2)}) collective-permute-start(bf16[40,128]{1,0:T(8,128)(2,1)S(1)} %get-tuple-element.26), channel_id=1, source_target_pairs={{0,8},{8,0},{16,24},{24,16},{1,9},{9,1},{17,25},{25,17},{2,10},{10... | collective-permute-start | bytes 30728 | tf_op jit(solution)/shard_map/ppermute | solution.py:47
  7.7 14.2 %collective-permute-start.3 = (bf16[40,128]{1,0:T(8,128)(2,1)S(1)}, bf16[40,128]{1,0:T(8,128)(2,1)S(1)}, u32[]{:S(2)}, u32[]{:S(2)}) collective-permute-start(bf16[40,128]{1,0:T(8,128)(2,1)S(1)} %get-tuple-element.27), channel_id=1, source_target_pairs={{8,16},{16,8},{9,17},{17,9},{10,18},{18,10},{11,19},{19,11},{12,20... | collective-permute-start | bytes 30728 | tf_op jit(solution)/shard_map/ppermute | solution.py:47
  11.2 10.6 %copy-start = (f32[32,128]{1,0:T(8,128)S(1)}, f32[32,128]{1,0:T(8,128)}, u32[]{:S(2)}) copy-start(f32[32,128]{1,0:T(8,128)} %get-tuple-element.28.refs_7_) | copy-start | bytes 49156
  21.8 11.6 %copy-start.5 = (f32[16,36]{1,0:T(8,128)S(1)}, f32[16,36]{1,0:T(8,128)}, u32[]{:S(2)}) copy-start(f32[16,36]{1,0:T(8,128)} %refs_0_.5) | copy-start | bytes 6916
  24.8 56.7 %all-to-all-start = ((bf16[32,248,128]{2,1,0:T(8,128)(2,1)}), bf16[32,248,128]{2,1,0:T(8,128)(2,1)S(1)}, u32[]{:S(2)}, u32[]{:S(2)}) async-start(bf16[32,248,128]{2,1,0:T(8,128)(2,1)} %get-tuple-element.31), calls=%async_computation | async-start | bytes 4063232 | tf_op jit(solution)/shard_map/all_to_all | solution.py:520
  86.6 3.2 %collective-permute-start.4 = (f32[16,128]{1,0:T(8,128)S(1)}, f32[16,128]{1,0:T(8,128)S(1)}, u32[]{:S(2)}, u32[]{:S(2)}) collective-permute-start(f32[16,128]{1,0:T(8,128)S(1)} %get-tuple-element.35), channel_id=1, source_target_pairs={{0,8},{8,0},{16,24},{24,16},{1,9},{9,1},{17,25},{25,17},{2,10},{10... | collective-permute-start | bytes 24584 | tf_op jit(solution)/shard_map/ppermute | solution.py:47
  87.4 5.0 %collective-permute-start.5 = (f32[16,128]{1,0:T(8,128)S(1)}, f32[16,128]{1,0:T(8,128)S(1)}, u32[]{:S(2)}, u32[]{:S(2)}) collective-permute-start(f32[16,128]{1,0:T(8,128)S(1)} %get-tuple-element.36), channel_id=1, source_target_pairs={{8,16},{16,8},{9,17},{17,9},{10,18},{18,10},{11,19},{19,11},{12,20... | collective-permute-start | bytes 24584 | tf_op jit(solution)/shard_map/ppermute | solution.py:47

commit v3 on v2

--- a/solution.py
+++ b/solution.py
@@ -81,14 +81,22 @@
 
 
 def first_kernel(
-    z, radar_l, radar_s, owner_l, slot_l, owner_s, slot_s, even_pairs, odd_pairs, base_l, base_s, marks
+    z, radar_l, radar_s, owner_l, slot_l, owner_s, slot_s, even_pairs, odd_pairs, base_l, base_s, marks,
+    held_l, held_s, arrived,
 ):
+    copies = [
+        pltpu.make_async_copy(source, held, arrived.at[k])
+        for k, (source, held) in enumerate(((radar_l, held_l), (radar_s, held_s)))
+    ]
+    for copy in copies:
+        copy.start()
     plan(z, owner_l, slot_l, owner_s, slot_s, base_l, base_s, marks)
     shape = (2 * SUB, COMPS * LANES)
     row, at = iota(shape, 0), iota(shape, 1)
     pick = ones_where(at == jnp.where(row < SUB, row * LANES, (row - SUB) * LANES + LANES - 1))
     start = 0
-    for radar, lines in ((radar_l, z.lines[0]), (radar_s, z.lines[1])):
+    for radar, lines, copy in zip((held_l, held_s), z.lines, copies):
+        copy.wait()
         rows = jnp.concatenate([radar[c] for c in range(COMPS)], axis=1)
         both = dot(pick, rows, NT)
         one, other = by_parity("swath", both[SUB:], both[0:SUB])
@@ -222,7 +230,7 @@
 
 def tail_kernel(
     z, base_l, base_s, given, sec_a, sec_b, swap_a, swap_b, marks,
-    lines_held, tiles_held, out, packed,
+    lines_held, tiles_held, sent, packed, out, leaving,
 ):
     del given
     tall = lines_held.shape[3]
@@ -275,6 +283,7 @@
     columns = [
         dot(pick, packed[o * z.stride : o * z.stride + z.lanes, :].astype(BF16), NT) for o in range(z.devices)
     ]
+    group, copies = z.devices // 4, []
     for o in range(z.devices):
         extra = jnp.broadcast_to(marks[o : o + 1, :], (SUB, LANES))
         one_less, one_more = max(o - 1, 0), min(o + 1, z.devices - 1)
@@ -284,6 +293,12 @@
             extra = jnp.where(row == 1 + steps + k, columns[one_more][:, part], extra)
         out[o, 0 : z.rows, :] = packed[o * z.stride : o * z.stride + z.rows, :].astype(BF16)
         out[o, z.rows :, :] = extra.astype(BF16)
+        if (o + 1) % group == 0:
+            part = pl.ds(o + 1 - group, group)
+            copies.append(pltpu.make_async_copy(out.at[part], sent.at[part], leaving.at[o // group]))
+            copies[-1].start()
+    for copy in copies:
+        copy.wait()
 
 
 def matrix_kernel(models, small, wide):
@@ -317,7 +332,7 @@
     return pick(0), pick(3)
 
 
-def merge_kernel(z, got, small, wide, out, even_pairs, odd_pairs, stage, extras, maps, fits):
+def merge_kernel(z, got, small, wide, maps, planes, even_pairs, odd_pairs, stage, extras, two):
     map_lines, n_model, devices = z.map_lines, z.n_model, z.devices
     steps = z.lanes // LANES
     for s in range(devices):
@@ -376,59 +391,70 @@
     at = iota((4 * n_model, n_model * LANES), 0) % (2 * n_model)
     to = iota((4 * n_model, n_model * LANES), 1)
     target = jnp.where(at < n_model, at * LANES + LANES - 1, (at - n_model) * LANES)
-    planes = dot(x, ones_where(to == target), TN)
-
-    matrix = wide[...]
-
-    def step(i, _):
-        halves = []
-        for h in range(2):
-            r = pl.multiple_of((2 * i + h) * SUB, SUB)
-            x = jnp.concatenate(coherency(*split_parts(lambda n: maps[n, pl.ds(r, SUB), :])), axis=0)
-            halves.append(x.astype(BF16))
-        result = dot(matrix, jnp.concatenate(halves, axis=1), NN)
-        result = result[0 : n_model * SUB] + result[n_model * SUB :]
-        for h in range(2):
-            r = pl.multiple_of((2 * i + h) * SUB, SUB)
+    planes[...] = dot(x, ones_where(to == target), TN)
+
+    ends = (0, map_lines - SUB)
+    two[...] = fit_block(wide, maps, ends, n_model)
+    for k in range(n_model):
+        part = slice(k * LANES, (k + 1) * LANES)
+        top = two[k * SUB : k * SUB + 1, 0:LANES]
+        bottom = two[k * SUB + SUB - 1 : (k + 1) * SUB, LANES:]
+        top = three_lanes(top, planes[0:1, part])
+        bottom = three_lanes(bottom, planes[map_lines - 1 : map_lines, part])
+        one, other = by_parity("sec", bottom, top)
+        even_pairs[k : k + 1, :] = one
+        odd_pairs[k : k + 1, :] = other
+
+
+def fit_block(wide, maps, starts, n_model):
+    halves = []
+    for r in starts:
+        x = jnp.concatenate(coherency(*split_parts(lambda n: maps[n, pl.ds(r, SUB), :])), axis=0)
+        halves.append(x.astype(BF16))
+    result = dot(wide[...], jnp.concatenate(halves, axis=1), NN)
+    return result[0 : n_model * SUB] + result[n_model * SUB :]
+
+
+def three_lanes(x, side):
+    lane = iota(x.shape, 1)
+    before = pltpu.roll(jnp.where(lane == LANES - 1, side, x), 1, 1)
+    after = pltpu.roll(jnp.where(lane == 0, side, x), LANES - 1, 1)
+    return x + before + after
+
+
+def spread_kernel(z, maps, planes, wide, out, ends, fits):
+    map_lines, n_model = z.map_lines, z.n_model
+    for i in range(map_lines // (2 * SUB)):
+        starts = (2 * i * SUB, (2 * i + 1) * SUB)
+        result = fit_block(wide, maps, starts, n_model)
+        for h, r in enumerate(starts):
             for k in range(n_model):
                 fits[k, pl.ds(SUB + r, SUB), :] = result[
                     k * SUB : (k + 1) * SUB, h * LANES : (h + 1) * LANES
                 ]
-        return _
-
-    lax.fori_loop(0, map_lines // (2 * SUB), step, 0, unroll=True)
     blank = jnp.zeros((1, LANES), F32)
     inner = pl.ds(SUB, map_lines)
     for k in range(n_model):
-        x = fits[k, inner, :]
-        side = planes[:, k * LANES : (k + 1) * LANES]
-        lane = iota(x.shape, 1)
-        before = pltpu.roll(jnp.where(lane == LANES - 1, side, x), 1, 1)
-        after = pltpu.roll(jnp.where(lane == 0, side, x), LANES - 1, 1)
-        x = x + before + after
+        x = three_lanes(fits[k, inner, :], planes[:, k * LANES : (k + 1) * LANES])
         fits[k, inner, :] = x
         fits[k, SUB - 1 : SUB, :] = blank
         fits[k, SUB + map_lines : SUB + map_lines + 1, :] = blank
-        one, other = by_parity("sec", x[map_lines - 1 :, :], x[0:1, :])
-        even_pairs[k : k + 1, :] = one
-        odd_pairs[k : k + 1, :] = other
-        out[k] = fits[k, pl.ds(SUB - 1, map_lines), :] + x + fits[k, pl.ds(SUB + 1, map_lines), :]
-
-
-def finish_kernel(z, given, sec_a, sec_b, out, ends, moving):
-    parts = (pl.ds(0, SUB), pl.ds(z.map_lines - SUB, SUB))
-    copies = [pltpu.make_async_copy(given.at[:, p, :], ends.at[k], moving.at[k]) for k, p in enumerate(parts)]
-    for copy in copies:
-        copy.start()
+        x = fits[k, pl.ds(SUB - 1, map_lines), :] + x + fits[k, pl.ds(SUB + 1, map_lines), :]
+        out[k] = x
+        ends[0, k] = x[0:SUB]
+        ends[1, k] = x[map_lines - SUB :]
+
+
+def finish_kernel(z, given, ends, sec_a, sec_b, out, held, moving):
+    del given
     below, above = by_parity("sec", sec_a[...], sec_b[...])
     line = iota((SUB, LANES), 0)
-    for copy in copies:
-        copy.wait()
-    copies = [pltpu.make_async_copy(ends.at[k], out.at[:, p, :], moving.at[2 + k]) for k, p in enumerate(parts)]
-    for end, (at, row) in enumerate(((0, above), (SUB - 1, below))):
+    copies = []
+    for end, (at, row, start) in enumerate(((0, above, 0), (SUB - 1, below, z.map_lines - SUB))):
         for k in range(z.n_model):
-            ends[end, k] = ends[end, k] + jnp.where(line == at, row[k : k + 1, :], 0.0)
-        copies[end].start()
+            held[end, k] = ends[end, k] + jnp.where(line == at, row[k : k + 1, :], 0.0)
+        copies.append(pltpu.make_async_copy(held.at[end], out.at[:, pl.ds(start, SUB), :], moving.at[end]))
+        copies[-1].start()
     for copy in copies:
         copy.wait()
 
@@ -469,9 +495,10 @@
     even, odd, base_l, base_s, marks = call_one(
         first_kernel,
         args,
-        [whole(x.shape) for x in args],
+        [ANY, ANY] + [whole(x.shape) for x in args[2:]],
         [column, column, shape((1, lines_l), jnp.int32), shape((1, lines_s), jnp.int32), shape((z.devices, LANES), F32)],
         58,
+        scratch=[pltpu.VMEM(x.shape, BF16) for x in radar] + [pltpu.SemaphoreType.DMA((2,))],
         flops=10_000_000_000,
         size=1_000_000,
     )
@@ -512,8 +539,9 @@
     sent, _ = pl.pallas_call(
         lambda *refs: tail_kernel(z, *refs),
         in_specs=[SMEM, SMEM] + [VMEM] * 8,
-        out_specs=[VMEM, VMEM],
+        out_specs=[ANY, VMEM],
         out_shape=[shape((z.devices, z.rows + SUB, LANES), BF16), buffer],
+        scratch_shapes=[pltpu.VMEM((z.devices, z.rows + SUB, LANES), BF16), pltpu.SemaphoreType.DMA((4,))],
         input_output_aliases={2: 1},
         compiler_params=params(24),
     )(*args)
@@ -526,30 +554,44 @@
         16, flops=50_000_000, size=1_000_000,
     )
     rim = shape((z.n_model, LANES), F32)
-    fit, even, odd = call(
+    maps, planes, even, odd = call(
         merge_kernel,
         (got, small, wide),
-        [shape((z.n_model, z.map_lines, LANES), F32), rim, rim],
-        32,
+        [
+            shape((2 * COMPS, z.map_lines, LANES), F32),
+            shape((z.map_lines, z.n_model * LANES), F32),
+            rim,
+            rim,
+        ],
+        24,
         scratch=[
             pltpu.VMEM((z.devices * max(z.caps), COMPS * LANES), F32),
             pltpu.VMEM((z.devices * SUB, LANES), F32),
-            pltpu.VMEM((2 * COMPS, z.map_lines, LANES), F32),
-            pltpu.VMEM((z.n_model, z.map_lines + 2 * SUB, LANES), F32),
+            pltpu.VMEM((z.n_model * SUB, 2 * LANES), F32),
         ],
         flops=1_000_000_000,
         size=4_000_000,
     )
     sec_a, sec_b = swap(even, odd, "sec")
+    edge = shape((2, z.n_model, SUB, LANES), F32)
+    fit, ends = call(
+        spread_kernel,
+        (maps, planes, wide),
+        [shape((z.n_model, z.map_lines, LANES), F32), edge],
+        24,
+        scratch=[pltpu.VMEM((z.n_model, z.map_lines + 2 * SUB, LANES), F32)],
+        flops=10_000_000_000,
+        size=4_000_000,
+    )
     return pl.pallas_call(
         lambda *refs: finish_kernel(z, *refs),
-        in_specs=[ANY, VMEM, VMEM],
+        in_specs=[ANY, VMEM, VMEM, VMEM],
         out_specs=ANY,
         out_shape=shape(fit.shape, F32),
-        scratch_shapes=[pltpu.VMEM((2, z.n_model, SUB, LANES), F32), pltpu.SemaphoreType.DMA((4,))],
+        scratch_shapes=[pltpu.VMEM(edge.shape, F32), pltpu.SemaphoreType.DMA((2,))],
         input_output_aliases={0: 0},
         compiler_params=params(16),
-    )(fit, sec_a, sec_b)
+    )(fit, ends, sec_a, sec_b)
 
 
 def solution(mesh):

time: 94.4 us -> 91.6 us (0.970)
  waiting for transfers between devices: 49.2 us -> 46.6 us
    ppermute x3, waiting for transfers between devices: 2.61 us -> 0.01 us  [swap(): lax.ppermute(odd_pairs, axis, pairs(1))]
    pallas_call x3 -> x4, Pallas kernels: 17.6 us -> 18.2 us  [call(): pl.pallas_call(lambda *refs: kernel(z, *refs) if kernel is not matrix_ker...]
  transfers between devices with their start and end apart: 7 -> 7, of which waited for: 3 -> 2; matrix products, arithmetic and copies ran while one was open for 0% -> 0% of each run, Pallas kernels for 13% -> 17%
where the time goes in v3:
time: 91.6 us; the launch traced here: 91.3 us
  waiting for transfers between devices  46.6 us (51%)
  Pallas kernels  24.7 us (27%)
  starting transfers between devices  19.8 us (22%)
    all_to_all x1, waiting for transfers between devices, body(): got = lax.all_to_all(sent, AXES, split_axis=0, concat_axis=0, tiled=True)  46.1 us
    pallas_call x4, Pallas kernels, call(): pl.pallas_call(lambda *refs: kernel(z, *refs) if kernel is not matrix_ker...  18.2 us
    all_to_all x1, starting transfers between devices, body(): got = lax.all_to_all(sent, AXES, split_axis=0, concat_axis=0, tiled=True)  8.6 us
    ppermute x3, starting transfers between devices, swap(): lax.ppermute(odd_pairs, axis, pairs(1))  6.64 us
    ppermute x3, starting transfers between devices, swap(): lax.ppermute(even_pairs, axis, pairs(0))  4.6 us
    pallas_call x2, Pallas kernels, call_one(): pl.pallas_call(lambda *refs: kernel(z, *refs), grid=(1,), in_specs=specs,...  3.17 us
    pallas_call x1, Pallas kernels, body(): pl.pallas_call(lambda *refs: tail_kernel(z, *refs), in_specs=[SMEM, SMEM]...  2.61 us
  transfers between devices with their start and end apart: 7, of which 2 were waited for; matrix products, arithmetic and copies ran while one was open for 0% of the time, Pallas kernels for 17%

profile of v3, /device:TPU:1, one launch (start us, length us, event | category | flops | bytes accessed | tf_op | source)
XLA Modules:
  0.0 91.3 jit_solution(11628379033858912217)
XLA Ops:
  0.0 3.1 %shard_map.91 = (bf16[8,640]{1,0:T(8,128)(2,1)}, bf16[8,640]{1,0:T(8,128)(2,1)}, s32[1,384]{1,0:T(1,128)}, s32[1,256]{1,0:T(1,128)}, f32[32,128]{1,0:T(8,128)}) custom-call(bf16[6,384,128]{2,1,0:T(8,128)(2,1)} %refs_2_.3, bf16[6,256,128]{2,1,0:T(8,128)(2,1)} %refs_3_.5, s32[1,384]{1,0:T(1,128)} %bitcast.2, s32[384]{0:T(512)} %refs_3_.3, s32[1,256]{1,0:T(1,128)} %bitcast.3, ...), custom_call_target="tpu_custom_call" | custom-call | flops 10000000000 | bytes 1000000 | tf_op jit(solution)/shard_map/pallas_call | solution.py:479
  3.1 2.1 %collective-permute-start = (bf16[8,640]{1,0:T(8,128)(2,1)}, bf16[8,640]{1,0:T(8,128)(2,1)S(1)}, u32[]{:S(2)}, u32[]{:S(2)}) collective-permute-start(bf16[8,640]{1,0:T(8,128)(2,1)} %get-tuple-element.26), channel_id=1, source_target_pairs={{0,1},{1,0},{2,3},{3,2},{4,5},{5,4},{6,7},{7,6},{8,9},{9,8},{10,11... | collective-permute-start | bytes 30728 | tf_op jit(solution)/shard_map/ppermute | solution.py:47
  5.2 0.8 collective-permute-start.1
  6.0 0.5 collective-permute-done.refs_4_.refs_5_
  6.5 0.0 collective-permute-done.1.refs_5_.refs_6_
  6.5 0.1 shard_map.93
  6.6 1.6 %collective-permute-start.2 = (bf16[40,128]{1,0:T(8,128)(2,1)S(1)}, bf16[40,128]{1,0:T(8,128)(2,1)S(1)}, u32[]{:S(2)}, u32[]{:S(2)}) collective-permute-start(bf16[40,128]{1,0:T(8,128)(2,1)S(1)} %get-tuple-element.29), channel_id=1, source_target_pairs={{0,8},{8,0},{16,24},{24,16},{1,9},{9,1},{17,25},{25,17},{2,10},{10... | collective-permute-start | bytes 30728 | tf_op jit(solution)/shard_map/ppermute | solution.py:47
  8.1 3.5 %collective-permute-start.3 = (bf16[40,128]{1,0:T(8,128)(2,1)S(1)}, bf16[40,128]{1,0:T(8,128)(2,1)S(1)}, u32[]{:S(2)}, u32[]{:S(2)}) collective-permute-start(bf16[40,128]{1,0:T(8,128)(2,1)S(1)} %get-tuple-element.30), channel_id=1, source_target_pairs={{8,16},{16,8},{9,17},{17,9},{10,18},{18,10},{11,19},{19,11},{12,20... | collective-permute-start | bytes 30728 | tf_op jit(solution)/shard_map/ppermute | solution.py:47
  11.7 0.0 copy-start
  11.7 10.6 %shard_map.92 = (f32[8336,128]{1,0:T(8,128)S(1)}, bf16[2,2,6,16,128]{4,3,2,1,0:T(8,128)(2,1)S(1)}, bf16[2,2,128,128]{3,2,1,0:T(8,128)(2,1)S(1)}) custom-call(s32[1,384]{1,0:T(1,128)S(1)} %copy-done.1, s32[1,256]{1,0:T(1,128)S(1)} %copy-done.2, bf16[6,384,128]{2,1,0:T(8,128)(2,1)S(1)} %copy-done.3, bf16[6,256,128]{2,1,0:T(8,128)(2,1)S(1)} %copy-done.4, ...), custom_call_target="tpu_custom_call" | custom-call | flops 10000000000 | bytes 20971520 | tf_op jit(solution)/shard_map/pallas_call | solution.py:468
  22.3 0.0 collective-permute-done.2.refs_3_
  22.3 0.0 collective-permute-done.3.refs_4_
  22.3 2.6 %shard_map.94 = (bf16[32,248,128]{2,1,0:T(8,128)(2,1)}, f32[8336,128]{1,0:T(8,128)S(1)}) custom-call(s32[1,384]{1,0:T(1,128)S(1)} %copy-done.1, s32[1,256]{1,0:T(1,128)S(1)} %copy-done.2, f32[8336,128]{1,0:T(8,128)S(1)} %get-tuple-element.28.refs_2_, bf16[40,128]{1,0:T(8,128)(2,1)S(1)} %collective-permute-done.2.refs_3_, ...), custom_call_target="tpu_custom_call", output_to_operand_aliasing={{1}: (2, {})} | custom-call | tf_op jit(solution)/shard_map/pallas_call | solution.py:539
  24.9 0.0 copy-start.5
  24.9 8.6 %all-to-all-start = ((bf16[32,248,128]{2,1,0:T(8,128)(2,1)}), bf16[32,248,128]{2,1,0:T(8,128)(2,1)S(1)}, u32[]{:S(2)}, u32[]{:S(2)}) async-start(bf16[32,248,128]{2,1,0:T(8,128)(2,1)} %get-tuple-element.34), calls=%async_computation | async-start | bytes 4063232 | tf_op jit(solution)/shard_map/all_to_all | solution.py:548
  33.6 1.9 %shard_map.95 = (f32[16,36]{1,0:T(8,128)S(1)}, bf16[256,288]{1,0:T(8,128)(2,1)S(1)}) custom-call(f32[16,36]{1,0:T(8,128)S(1)} %copy-done.5), custom_call_target="tpu_custom_call" | custom-call | flops 50000000 | bytes 1000000 | tf_op jit(solution)/shard_map/pallas_call | solution.py:468
  35.5 46.1 %all-to-all-done.refs_0_ = bf16[32,248,128]{2,1,0:T(8,128)(2,1)S(1)} async-done(((bf16[32,248,128]{2,1,0:T(8,128)(2,1)}), bf16[32,248,128]{2,1,0:T(8,128)(2,1)S(1)}, u32[]{:S(2)}, u32[]{:S(2)}) %all-to-all-start) | async-done | bytes 2031648 | tf_op jit(solution)/shard_map/all_to_all | solution.py:548
  81.6 2.3 %shard_map.96 = (f32[12,256,128]{2,1,0:T(8,128)S(1)}, f32[256,2048]{1,0:T(8,128)S(1)}, f32[16,128]{1,0:T(8,128)S(1)}, f32[16,128]{1,0:T(8,128)S(1)}) custom-call(bf16[32,248,128]{2,1,0:T(8,128)(2,1)S(1)} %all-to-all-done.refs_0_, f32[16,36]{1,0:T(8,128)S(1)} %get-tuple-element.35.refs_1_, bf16[256,288]{1,0:T(8,128)(2,1)S(1)} %get-tuple-element.36.refs_2_), custom_call_target="tpu_custom_call" | custom-call | flops 1000000000 | bytes 4000000 | tf_op jit(solution)/shard_map/pallas_call | solution.py:468
  83.9 0.9 %collective-permute-start.4 = (f32[16,128]{1,0:T(8,128)S(1)}, f32[16,128]{1,0:T(8,128)S(1)}, u32[]{:S(2)}, u32[]{:S(2)}) collective-permute-start(f32[16,128]{1,0:T(8,128)S(1)} %get-tuple-element.41), channel_id=1, source_target_pairs={{0,8},{8,0},{16,24},{24,16},{1,9},{9,1},{17,25},{25,17},{2,10},{10... | collective-permute-start | bytes 24584 | tf_op jit(solution)/shard_map/ppermute | solution.py:47
  84.8 2.3 %collective-permute-start.5 = (f32[16,128]{1,0:T(8,128)S(1)}, f32[16,128]{1,0:T(8,128)S(1)}, u32[]{:S(2)}, u32[]{:S(2)}) collective-permute-start(f32[16,128]{1,0:T(8,128)S(1)} %get-tuple-element.42), channel_id=1, source_target_pairs={{8,16},{16,8},{9,17},{17,9},{10,18},{18,10},{11,19},{19,11},{12,20... | collective-permute-start | bytes 24584 | tf_op jit(solution)/shard_map/ppermute | solution.py:47
  87.2 3.4 %shard_map.97 = (f32[16,256,128]{2,1,0:T(8,128)}, f32[2,16,8,128]{3,2,1,0:T(8,128)S(1)}) custom-call(f32[12,256,128]{2,1,0:T(8,128)S(1)} %get-tuple-element.37.refs_0_, f32[256,2048]{1,0:T(8,128)S(1)} %get-tuple-element.38.refs_1_, bf16[256,288]{1,0:T(8,128)(2,1)S(1)} %get-tuple-element.36.refs_2_), custom_call_target="tpu_custom_call" | custom-call | flops 10000000000 | bytes 4000000 | tf_op jit(solution)/shard_map/pallas_call | solution.py:468
  90.6 0.0 collective-permute-done.4.refs_2_
  90.6 0.0 collective-permute-done.5.refs_3_
  90.6 0.7 shard_map.98
  (10 shorter events, 0.0 us)
Async XLA Ops:
  0.0 6.5 %copy-start.3 = (bf16[6,384,128]{2,1,0:T(8,128)(2,1)S(1)}, bf16[6,384,128]{2,1,0:T(8,128)(2,1)}, u32[]{:S(2)}) copy-start(bf16[6,384,128]{2,1,0:T(8,128)(2,1)} %refs_2_.3) | copy-start | bytes 1769476
  0.0 6.5 %copy-start.4 = (bf16[6,256,128]{2,1,0:T(8,128)(2,1)S(1)}, bf16[6,256,128]{2,1,0:T(8,128)(2,1)}, u32[]{:S(2)}) copy-start(bf16[6,256,128]{2,1,0:T(8,128)(2,1)} %refs_3_.5) | copy-start | bytes 1179652
  3.1 3.4 %collective-permute-start = (bf16[8,640]{1,0:T(8,128)(2,1)}, bf16[8,640]{1,0:T(8,128)(2,1)S(1)}, u32[]{:S(2)}, u32[]{:S(2)}) collective-permute-start(bf16[8,640]{1,0:T(8,128)(2,1)} %get-tuple-element.26), channel_id=1, source_target_pairs={{0,1},{1,0},{2,3},{3,2},{4,5},{5,4},{6,7},{7,6},{8,9},{9,8},{10,11... | collective-permute-start | bytes 30728 | tf_op jit(solution)/shard_map/ppermute | solution.py:47
  5.2 6.5 %copy-start.1 = (s32[1,384]{1,0:T(1,128)S(1)}, s32[1,384]{1,0:T(1,128)}, u32[]{:S(2)}) copy-start(s32[1,384]{1,0:T(1,128)} %get-tuple-element.24.refs_0_) | copy-start | bytes 4612
  5.2 6.5 %copy-start.2 = (s32[1,256]{1,0:T(1,128)S(1)}, s32[1,256]{1,0:T(1,128)}, u32[]{:S(2)}) copy-start(s32[1,256]{1,0:T(1,128)} %get-tuple-element.25.refs_1_) | copy-start | bytes 3076
  5.2 1.3 %collective-permute-start.1 = (bf16[8,640]{1,0:T(8,128)(2,1)}, bf16[8,640]{1,0:T(8,128)(2,1)S(1)}, u32[]{:S(2)}, u32[]{:S(2)}) collective-permute-start(bf16[8,640]{1,0:T(8,128)(2,1)} %get-tuple-element.27), channel_id=1, source_target_pairs={{1,2},{2,1},{3,4},{4,3},{5,6},{6,5},{9,10},{10,9},{11,12},{12,11},... | collective-permute-start | bytes 30728 | tf_op jit(solution)/shard_map/ppermute | solution.py:47
  6.6 15.7 %collective-permute-start.2 = (bf16[40,128]{1,0:T(8,128)(2,1)S(1)}, bf16[40,128]{1,0:T(8,128)(2,1)S(1)}, u32[]{:S(2)}, u32[]{:S(2)}) collective-permute-start(bf16[40,128]{1,0:T(8,128)(2,1)S(1)} %get-tuple-element.29), channel_id=1, source_target_pairs={{0,8},{8,0},{16,24},{24,16},{1,9},{9,1},{17,25},{25,17},{2,10},{10... | collective-permute-start | bytes 30728 | tf_op jit(solution)/shard_map/ppermute | solution.py:47
  8.1 14.2 %collective-permute-start.3 = (bf16[40,128]{1,0:T(8,128)(2,1)S(1)}, bf16[40,128]{1,0:T(8,128)(2,1)S(1)}, u32[]{:S(2)}, u32[]{:S(2)}) collective-permute-start(bf16[40,128]{1,0:T(8,128)(2,1)S(1)} %get-tuple-element.30), channel_id=1, source_target_pairs={{8,16},{16,8},{9,17},{17,9},{10,18},{18,10},{11,19},{19,11},{12,20... | collective-permute-start | bytes 30728 | tf_op jit(solution)/shard_map/ppermute | solution.py:47
  11.7 10.6 %copy-start = (f32[32,128]{1,0:T(8,128)S(1)}, f32[32,128]{1,0:T(8,128)}, u32[]{:S(2)}) copy-start(f32[32,128]{1,0:T(8,128)} %get-tuple-element.31.refs_7_) | copy-start | bytes 49156
  24.9 8.6 %copy-start.5 = (f32[16,36]{1,0:T(8,128)S(1)}, f32[16,36]{1,0:T(8,128)}, u32[]{:S(2)}) copy-start(f32[16,36]{1,0:T(8,128)} %refs_0_.5) | copy-start | bytes 6916
  24.9 56.7 %all-to-all-start = ((bf16[32,248,128]{2,1,0:T(8,128)(2,1)}), bf16[32,248,128]{2,1,0:T(8,128)(2,1)S(1)}, u32[]{:S(2)}, u32[]{:S(2)}) async-start(bf16[32,248,128]{2,1,0:T(8,128)(2,1)} %get-tuple-element.34), calls=%async_computation | async-start | bytes 4063232 | tf_op jit(solution)/shard_map/all_to_all | solution.py:548
  83.9 6.7 %collective-permute-start.4 = (f32[16,128]{1,0:T(8,128)S(1)}, f32[16,128]{1,0:T(8,128)S(1)}, u32[]{:S(2)}, u32[]{:S(2)}) collective-permute-start(f32[16,128]{1,0:T(8,128)S(1)} %get-tuple-element.41), channel_id=1, source_target_pairs={{0,8},{8,0},{16,24},{24,16},{1,9},{9,1},{17,25},{25,17},{2,10},{10... | collective-permute-start | bytes 24584 | tf_op jit(solution)/shard_map/ppermute | solution.py:47
  84.8 5.8 %collective-permute-start.5 = (f32[16,128]{1,0:T(8,128)S(1)}, f32[16,128]{1,0:T(8,128)S(1)}, u32[]{:S(2)}, u32[]{:S(2)}) collective-permute-start(f32[16,128]{1,0:T(8,128)S(1)} %get-tuple-element.42), channel_id=1, source_target_pairs={{8,16},{16,8},{9,17},{17,9},{10,18},{18,10},{11,19},{19,11},{12,20... | collective-permute-start | bytes 24584 | tf_op jit(solution)/shard_map/ppermute | solution.py:47

commit v4 on v3

--- a/solution.py
+++ b/solution.py
@@ -156,28 +156,32 @@
     return before, after
 
 
-def filter_band(tiles, radar, left, right, work, filtered):
+def filter_planes(tiles, radar, left, right, planes):
     inner = pl.ds(SUB, tiles)
     blank = jnp.zeros((1, LANES), F32)
-    for plane in range(3):
-        work[plane, SUB - 1 : SUB, :] = blank
-        work[plane, SUB + tiles : SUB + tiles + 1, :] = blank
-    body = [radar[c].astype(F32) for c in range(COMPS)]
+    for plane in range(3 + COMPS):
+        planes[plane, SUB - 1 : SUB, :] = blank
+        planes[plane, SUB + tiles : SUB + tiles + 1, :] = blank
+    squares = lambda values: sum(v * v for v in values)
     lefts = [left[:, c : c + 1] for c in range(COMPS)]
     rights = [right[:, c : c + 1] for c in range(COMPS)]
-    squares = lambda values: sum(v * v for v in values)
-    power = squares(body)
-    for plane, value in enumerate((power,) + with_sides(power, squares(lefts), squares(rights))):
-        work[plane, inner, :] = value
-    near = [work[plane, pl.ds(SUB + d, tiles), :] for plane in range(3) for d in (-1, 0, 1)]
-    gain = gain_of(near)
+    total = jnp.zeros((tiles, LANES), F32)
     for c in range(COMPS):
-        plane = c % 3
-        before, after = with_sides(body[c], lefts[c], rights[c])
-        work[plane, inner, :] = body[c] + before + after
-        mean = work[plane, pl.ds(SUB - 1, tiles), :] + work[plane, inner, :]
-        mean = (mean + work[plane, pl.ds(SUB + 1, tiles), :]) / 9.0
-        filtered[pl.ds(c, tiles, stride=SUB), :] = mean + gain * (body[c] - mean)
+        x = radar[c].astype(F32)
+        total = total + x * x
+        before, after = with_sides(x, lefts[c], rights[c])
+        planes[3 + c, inner, :] = x + before + after
+    for plane, value in enumerate((total,) + with_sides(total, squares(lefts), squares(rights))):
+        planes[plane, inner, :] = value
+
+
+def filter_lines(start, lines, radar, planes, filtered):
+    at = lambda plane, shift: planes[plane, pl.ds(SUB + start + shift, lines), :]
+    gain = gain_of([at(plane, d) for plane in range(3) for d in (-1, 0, 1)])
+    for c in range(COMPS):
+        mean = (at(3 + c, -1) + at(3 + c, 0) + at(3 + c, 1)) / 9.0
+        x = radar[c, pl.ds(start, lines), :].astype(F32)
+        filtered[pl.ds(start * SUB + c, lines, stride=SUB), :] = mean + gain * (x - mean)
 
 
 def gain_of(near):
@@ -191,17 +195,13 @@
 
 def send_kernel(
     z, base_l, base_s, radar_l, radar_s, swap_a, swap_b, weights_l, weights_s,
-    packed, edge_lines, edge_tiles, work, filtered, held_l, held_s, arrived,
+    packed, edge_lines, edge_tiles, planes_l, planes_s, filtered_l, filtered_s, held_l, arrived,
 ):
-    chunks, count = [], 0
-    for source, held, lines in ((weights_l, held_l, z.lines[0]), (weights_s, held_s, z.lines[1])):
-        copies = []
-        for at in range(0, lines, z.part):
-            part = pl.ds(at, z.part)
-            copies.append(pltpu.make_async_copy(source.at[part], held.at[part], arrived.at[count]))
-            copies[-1].start()
-            count += 1
-        chunks.append(copies)
+    copies = []
+    for at in range(0, z.lines[0], z.part):
+        part = pl.ds(at, z.part)
+        copies.append(pltpu.make_async_copy(weights_l.at[part], held_l.at[part], arrived.at[len(copies)]))
+        copies[-1].start()
     packed[...] = jnp.zeros_like(packed)
     tall = edge_lines.shape[3]
     for band, radar in enumerate((radar_l, radar_s)):
@@ -209,23 +209,38 @@
         edge_lines[band, 1] = radar[:, z.lines[band] - tall :, :]
     after, before = by_parity("swath", swap_a[...].astype(F32), swap_b[...].astype(F32))
     left, right = before.T, after.T
-    at = 0
-    for band, (radar, base, held) in enumerate(((radar_l, base_l, held_l), (radar_s, base_s, held_s))):
-        tiles, capacity = z.lines[band], z.caps[band]
-        filter_band(tiles, radar, left[at : at + tiles], right[at : at + tiles], work, filtered)
-        at += tiles
-        for i, copy in enumerate(chunks[band]):
-            copy.wait()
-            for t in range(0, z.part, 2):
-                tile = i * z.part + t
-                lines = filtered[pl.ds(tile * SUB, 2 * SUB), :].astype(BF16)
-                matrix = held[pl.ds(tile, 2)].reshape(2 * LANES, LANES)
-                result = dot(lines, matrix, NT)
-                first, second = base[0, tile], base[0, tile + 1]
-                packed[pl.ds(first, COMPS, stride=capacity), :] = result[0:COMPS, 0:LANES]
-                packed[pl.ds(second, COMPS, stride=capacity), :] = result[SUB : SUB + COMPS, LANES:]
+    bands = (
+        (radar_l, base_l, held_l, planes_l, filtered_l),
+        (radar_s, base_s, weights_s, planes_s, filtered_s),
+    )
+    at = (0, z.lines[0])
+    for band in (1, 0):
+        radar, _, _, planes, _ = bands[band]
+        part = slice(at[band], at[band] + z.lines[band])
+        filter_planes(z.lines[band], radar, left[part], right[part], planes)
+    todo = [(band, start) for band in (1, 0) for start in range(0, z.lines[band], z.part)]
+
+    def lines_of(band, start):
+        radar, _, _, planes, filtered = bands[band]
+        filter_lines(start, z.part, radar, planes, filtered)
+
+    lines_of(*todo[0])
+    for i, (band, start) in enumerate(todo):
+        _, base, held, _, filtered = bands[band]
+        if band == 0:
+            copies[start // z.part].wait()
+        if i + 1 < len(todo):
+            lines_of(*todo[i + 1])
+        for tile in range(start, start + z.part, 2):
+            lines = filtered[pl.ds(tile * SUB, 2 * SUB), :].astype(BF16)
+            matrix = held[pl.ds(tile, 2)].reshape(2 * LANES, LANES)
+            result = dot(lines, matrix, NT)
+            first, second = base[0, tile], base[0, tile + 1]
+            packed[pl.ds(first, COMPS, stride=z.caps[band]), :] = result[0:COMPS, 0:LANES]
+            packed[pl.ds(second, COMPS, stride=z.caps[band]), :] = result[SUB : SUB + COMPS, LANES:]
+    for band, (_, _, held, _, _) in enumerate(bands):
         edge_tiles[band, 0] = held[0]
-        edge_tiles[band, 1] = held[tiles - 1]
+        edge_tiles[band, 1] = held[z.lines[band] - 1]
 
 
 def tail_kernel(
@@ -511,7 +526,7 @@
     edges = [edge(lines, end) for end in range(2) for lines in z.lines]
     side = whole(column.shape)
     even, odd = call_one(
-        second_kernel, radar * 2 + (swap_a, swap_b), edges + [side, side], [strip, strip], 32, flops=10_000_000_000, size=1_000_000,
+        second_kernel, radar * 2 + (swap_a, swap_b), edges + [side, side], [strip, strip], 16, flops=1_000_000_000_000, size=1_000_000,
     )
     sec_a, sec_b = swap(even, odd, "sec")
     buffer = shape((z.devices * z.stride + up_to(COMPS * max(z.caps), SUB), LANES), F32)
@@ -523,14 +538,13 @@
             shape((2, 2, COMPS, tall, LANES), BF16),
             shape((2, 2, LANES, LANES), BF16),
         ],
-        44,
-        specs=[SMEM, SMEM] + [VMEM] * 4 + [ANY] * 2,
+        34,
+        specs=[SMEM, SMEM] + [VMEM] * 4 + [ANY, VMEM],
         scratch=[
-            pltpu.VMEM((3, max(z.lines) + 2 * SUB, LANES), F32),
-            pltpu.VMEM((max(z.lines) * SUB, LANES), F32),
+            *[pltpu.VMEM((3 + COMPS, n + 2 * SUB, LANES), F32) for n in z.lines],
+            *[pltpu.VMEM((n * SUB, LANES), F32) for n in z.lines],
             pltpu.VMEM(weights_l.shape, BF16),
-            pltpu.VMEM(weights_s.shape, BF16),
-            pltpu.SemaphoreType.DMA((sum(z.lines) // z.part,)),
+            pltpu.SemaphoreType.DMA((lines_l // z.part,)),
         ],
         flops=10_000_000_000,
         size=2 * (weights_l.size + weights_s.size),

time: 91.6 us -> 92.2 us (level)
  no operation moved by 1% of the time
where the time goes in v4:
time: 92.2 us; the launch traced here: 91.9 us
  waiting for transfers between devices  46.7 us (51%)
  Pallas kernels  24.8 us (27%)
  starting transfers between devices  20.2 us (22%)
    all_to_all x1, waiting for transfers between devices, body(): got = lax.all_to_all(sent, AXES, split_axis=0, concat_axis=0, tiled=True)  46.1 us
    pallas_call x4, Pallas kernels, call(): pl.pallas_call(lambda *refs: kernel(z, *refs) if kernel is not matrix_ker...  18.3 us
    all_to_all x1, starting transfers between devices, body(): got = lax.all_to_all(sent, AXES, split_axis=0, concat_axis=0, tiled=True)  8.85 us
    ppermute x3, starting transfers between devices, swap(): lax.ppermute(odd_pairs, axis, pairs(1))  6.77 us
    ppermute x3, starting transfers between devices, swap(): lax.ppermute(even_pairs, axis, pairs(0))  4.59 us
    pallas_call x2, Pallas kernels, call_one(): pl.pallas_call(lambda *refs: kernel(z, *refs), grid=(1,), in_specs=specs,...  3.17 us
    pallas_call x1, Pallas kernels, body(): pl.pallas_call(lambda *refs: tail_kernel(z, *refs), in_specs=[SMEM, SMEM]...  2.61 us
  transfers between devices with their start and end apart: 7, of which 2 were waited for; matrix products, arithmetic and copies ran while one was open for 0% of the time, Pallas kernels for 17%

profile of v4, /device:TPU:1, one launch (start us, length us, event | category | flops | bytes accessed | tf_op | source)
XLA Modules:
  0.0 91.9 jit_solution(13362760497317181071)
XLA Ops:
  0.0 3.1 %shard_map.91 = (bf16[8,640]{1,0:T(8,128)(2,1)}, bf16[8,640]{1,0:T(8,128)(2,1)}, s32[1,384]{1,0:T(1,128)}, s32[1,256]{1,0:T(1,128)}, f32[32,128]{1,0:T(8,128)}) custom-call(bf16[6,384,128]{2,1,0:T(8,128)(2,1)} %refs_2_.3, bf16[6,256,128]{2,1,0:T(8,128)(2,1)} %refs_3_.5, s32[1,384]{1,0:T(1,128)} %bitcast.2, s32[384]{0:T(512)} %refs_3_.3, s32[1,256]{1,0:T(1,128)} %bitcast.3, ...), custom_call_target="tpu_custom_call" | custom-call | flops 10000000000 | bytes 1000000 | tf_op jit(solution)/shard_map/pallas_call | solution.py:494
  3.1 2.1 %collective-permute-start = (bf16[8,640]{1,0:T(8,128)(2,1)}, bf16[8,640]{1,0:T(8,128)(2,1)S(1)}, u32[]{:S(2)}, u32[]{:S(2)}) collective-permute-start(bf16[8,640]{1,0:T(8,128)(2,1)} %get-tuple-element.26), channel_id=1, source_target_pairs={{0,1},{1,0},{2,3},{3,2},{4,5},{5,4},{6,7},{7,6},{8,9},{9,8},{10,11... | collective-permute-start | bytes 30728 | tf_op jit(solution)/shard_map/ppermute | solution.py:47
  5.2 0.7 collective-permute-start.1
  5.9 0.6 collective-permute-done.refs_4_.refs_5_
  6.5 0.0 collective-permute-done.1.refs_5_.refs_6_
  6.5 0.0 copy-start.3
  6.5 0.1 shard_map.93
  6.6 1.6 %collective-permute-start.2 = (bf16[40,128]{1,0:T(8,128)(2,1)S(1)}, bf16[40,128]{1,0:T(8,128)(2,1)S(1)}, u32[]{:S(2)}, u32[]{:S(2)}) collective-permute-start(bf16[40,128]{1,0:T(8,128)(2,1)S(1)} %get-tuple-element.29), channel_id=1, source_target_pairs={{0,8},{8,0},{16,24},{24,16},{1,9},{9,1},{17,25},{25,17},{2,10},{10... | collective-permute-start | bytes 30728 | tf_op jit(solution)/shard_map/ppermute | solution.py:47
  8.2 3.8 %collective-permute-start.3 = (bf16[40,128]{1,0:T(8,128)(2,1)S(1)}, bf16[40,128]{1,0:T(8,128)(2,1)S(1)}, u32[]{:S(2)}, u32[]{:S(2)}) collective-permute-start(bf16[40,128]{1,0:T(8,128)(2,1)S(1)} %get-tuple-element.30), channel_id=1, source_target_pairs={{8,16},{16,8},{9,17},{17,9},{10,18},{18,10},{11,19},{19,11},{12,20... | collective-permute-start | bytes 30728 | tf_op jit(solution)/shard_map/ppermute | solution.py:47
  12.0 0.0 copy-start
  12.0 10.6 %shard_map.92 = (f32[8336,128]{1,0:T(8,128)S(1)}, bf16[2,2,6,16,128]{4,3,2,1,0:T(8,128)(2,1)S(1)}, bf16[2,2,128,128]{3,2,1,0:T(8,128)(2,1)S(1)}) custom-call(s32[1,384]{1,0:T(1,128)S(1)} %copy-done.1, s32[1,256]{1,0:T(1,128)S(1)} %copy-done.2, bf16[6,384,128]{2,1,0:T(8,128)(2,1)S(1)} %copy-done.4, bf16[6,256,128]{2,1,0:T(8,128)(2,1)S(1)} %copy-done.5, ...), custom_call_target="tpu_custom_call" | custom-call | flops 10000000000 | bytes 20971520 | tf_op jit(solution)/shard_map/pallas_call | solution.py:483
  22.7 0.0 collective-permute-done.2.refs_3_
  22.7 0.0 collective-permute-done.3.refs_4_
  22.7 2.6 %shard_map.94 = (bf16[32,248,128]{2,1,0:T(8,128)(2,1)}, f32[8336,128]{1,0:T(8,128)S(1)}) custom-call(s32[1,384]{1,0:T(1,128)S(1)} %copy-done.1, s32[1,256]{1,0:T(1,128)S(1)} %copy-done.2, f32[8336,128]{1,0:T(8,128)S(1)} %get-tuple-element.28.refs_2_, bf16[40,128]{1,0:T(8,128)(2,1)S(1)} %collective-permute-done.2.refs_3_, ...), custom_call_target="tpu_custom_call", output_to_operand_aliasing={{1}: (2, {})} | custom-call | tf_op jit(solution)/shard_map/pallas_call | solution.py:553
  25.3 0.0 copy-start.6
  25.3 8.9 %all-to-all-start = ((bf16[32,248,128]{2,1,0:T(8,128)(2,1)}), bf16[32,248,128]{2,1,0:T(8,128)(2,1)S(1)}, u32[]{:S(2)}, u32[]{:S(2)}) async-start(bf16[32,248,128]{2,1,0:T(8,128)(2,1)} %get-tuple-element.34), calls=%async_computation | async-start | bytes 4063232 | tf_op jit(solution)/shard_map/all_to_all | solution.py:562
  34.2 1.9 %shard_map.95 = (f32[16,36]{1,0:T(8,128)S(1)}, bf16[256,288]{1,0:T(8,128)(2,1)S(1)}) custom-call(f32[16,36]{1,0:T(8,128)S(1)} %copy-done.6), custom_call_target="tpu_custom_call" | custom-call | flops 50000000 | bytes 1000000 | tf_op jit(solution)/shard_map/pallas_call | solution.py:483
  36.1 46.1 %all-to-all-done.refs_0_ = bf16[32,248,128]{2,1,0:T(8,128)(2,1)S(1)} async-done(((bf16[32,248,128]{2,1,0:T(8,128)(2,1)}), bf16[32,248,128]{2,1,0:T(8,128)(2,1)S(1)}, u32[]{:S(2)}, u32[]{:S(2)}) %all-to-all-start) | async-done | bytes 2031648 | tf_op jit(solution)/shard_map/all_to_all | solution.py:562
  82.2 2.3 %shard_map.96 = (f32[12,256,128]{2,1,0:T(8,128)S(1)}, f32[256,2048]{1,0:T(8,128)S(1)}, f32[16,128]{1,0:T(8,128)S(1)}, f32[16,128]{1,0:T(8,128)S(1)}) custom-call(bf16[32,248,128]{2,1,0:T(8,128)(2,1)S(1)} %all-to-all-done.refs_0_, f32[16,36]{1,0:T(8,128)S(1)} %get-tuple-element.35.refs_1_, bf16[256,288]{1,0:T(8,128)(2,1)S(1)} %get-tuple-element.36.refs_2_), custom_call_target="tpu_custom_call" | custom-call | flops 1000000000 | bytes 4000000 | tf_op jit(solution)/shard_map/pallas_call | solution.py:483
  84.6 0.9 collective-permute-start.4
  85.5 2.3 %collective-permute-start.5 = (f32[16,128]{1,0:T(8,128)S(1)}, f32[16,128]{1,0:T(8,128)S(1)}, u32[]{:S(2)}, u32[]{:S(2)}) collective-permute-start(f32[16,128]{1,0:T(8,128)S(1)} %get-tuple-element.42), channel_id=1, source_target_pairs={{8,16},{16,8},{9,17},{17,9},{10,18},{18,10},{11,19},{19,11},{12,20... | collective-permute-start | bytes 24584 | tf_op jit(solution)/shard_map/ppermute | solution.py:47
  87.8 3.4 %shard_map.97 = (f32[16,256,128]{2,1,0:T(8,128)}, f32[2,16,8,128]{3,2,1,0:T(8,128)S(1)}) custom-call(f32[12,256,128]{2,1,0:T(8,128)S(1)} %get-tuple-element.37.refs_0_, f32[256,2048]{1,0:T(8,128)S(1)} %get-tuple-element.38.refs_1_, bf16[256,288]{1,0:T(8,128)(2,1)S(1)} %get-tuple-element.36.refs_2_), custom_call_target="tpu_custom_call" | custom-call | flops 10000000000 | bytes 4000000 | tf_op jit(solution)/shard_map/pallas_call | solution.py:483
  91.2 0.0 collective-permute-done.4.refs_2_
  91.2 0.7 shard_map.98
  (12 shorter events, 0.0 us)
Async XLA Ops:
  0.0 6.5 %copy-start.4 = (bf16[6,384,128]{2,1,0:T(8,128)(2,1)S(1)}, bf16[6,384,128]{2,1,0:T(8,128)(2,1)}, u32[]{:S(2)}) copy-start(bf16[6,384,128]{2,1,0:T(8,128)(2,1)} %refs_2_.3) | copy-start | bytes 1769476
  0.0 6.5 %copy-start.5 = (bf16[6,256,128]{2,1,0:T(8,128)(2,1)S(1)}, bf16[6,256,128]{2,1,0:T(8,128)(2,1)}, u32[]{:S(2)}) copy-start(bf16[6,256,128]{2,1,0:T(8,128)(2,1)} %refs_3_.5) | copy-start | bytes 1179652
  3.1 3.4 %collective-permute-start = (bf16[8,640]{1,0:T(8,128)(2,1)}, bf16[8,640]{1,0:T(8,128)(2,1)S(1)}, u32[]{:S(2)}, u32[]{:S(2)}) collective-permute-start(bf16[8,640]{1,0:T(8,128)(2,1)} %get-tuple-element.26), channel_id=1, source_target_pairs={{0,1},{1,0},{2,3},{3,2},{4,5},{5,4},{6,7},{7,6},{8,9},{9,8},{10,11... | collective-permute-start | bytes 30728 | tf_op jit(solution)/shard_map/ppermute | solution.py:47
  5.2 1.3 %collective-permute-start.1 = (bf16[8,640]{1,0:T(8,128)(2,1)}, bf16[8,640]{1,0:T(8,128)(2,1)S(1)}, u32[]{:S(2)}, u32[]{:S(2)}) collective-permute-start(bf16[8,640]{1,0:T(8,128)(2,1)} %get-tuple-element.27), channel_id=1, source_target_pairs={{1,2},{2,1},{3,4},{4,3},{5,6},{6,5},{9,10},{10,9},{11,12},{12,11},... | collective-permute-start | bytes 30728 | tf_op jit(solution)/shard_map/ppermute | solution.py:47
  6.5 5.5 %copy-start.1 = (s32[1,384]{1,0:T(1,128)S(1)}, s32[1,384]{1,0:T(1,128)}, u32[]{:S(2)}) copy-start(s32[1,384]{1,0:T(1,128)} %get-tuple-element.24.refs_0_) | copy-start | bytes 4612
  6.5 5.5 %copy-start.2 = (s32[1,256]{1,0:T(1,128)S(1)}, s32[1,256]{1,0:T(1,128)}, u32[]{:S(2)}) copy-start(s32[1,256]{1,0:T(1,128)} %get-tuple-element.25.refs_1_) | copy-start | bytes 3076
  6.5 5.5 %copy-start.3 = (bf16[256,128,128]{2,1,0:T(8,128)(2,1)S(1)}, bf16[256,128,128]{2,1,0:T(8,128)(2,1)}, u32[]{:S(2)}) copy-start(bf16[256,128,128]{2,1,0:T(8,128)(2,1)} %refs_7_.1) | copy-start | bytes 25165828
  6.6 16.0 %collective-permute-start.2 = (bf16[40,128]{1,0:T(8,128)(2,1)S(1)}, bf16[40,128]{1,0:T(8,128)(2,1)S(1)}, u32[]{:S(2)}, u32[]{:S(2)}) collective-permute-start(bf16[40,128]{1,0:T(8,128)(2,1)S(1)} %get-tuple-element.29), channel_id=1, source_target_pairs={{0,8},{8,0},{16,24},{24,16},{1,9},{9,1},{17,25},{25,17},{2,10},{10... | collective-permute-start | bytes 30728 | tf_op jit(solution)/shard_map/ppermute | solution.py:47
  8.2 14.5 %collective-permute-start.3 = (bf16[40,128]{1,0:T(8,128)(2,1)S(1)}, bf16[40,128]{1,0:T(8,128)(2,1)S(1)}, u32[]{:S(2)}, u32[]{:S(2)}) collective-permute-start(bf16[40,128]{1,0:T(8,128)(2,1)S(1)} %get-tuple-element.30), channel_id=1, source_target_pairs={{8,16},{16,8},{9,17},{17,9},{10,18},{18,10},{11,19},{19,11},{12,20... | collective-permute-start | bytes 30728 | tf_op jit(solution)/shard_map/ppermute | solution.py:47
  12.0 10.7 %copy-start = (f32[32,128]{1,0:T(8,128)S(1)}, f32[32,128]{1,0:T(8,128)}, u32[]{:S(2)}) copy-start(f32[32,128]{1,0:T(8,128)} %get-tuple-element.31.refs_7_) | copy-start | bytes 49156
  25.3 8.9 %copy-start.6 = (f32[16,36]{1,0:T(8,128)S(1)}, f32[16,36]{1,0:T(8,128)}, u32[]{:S(2)}) copy-start(f32[16,36]{1,0:T(8,128)} %refs_0_.5) | copy-start | bytes 6916
  25.3 56.9 %all-to-all-start = ((bf16[32,248,128]{2,1,0:T(8,128)(2,1)}), bf16[32,248,128]{2,1,0:T(8,128)(2,1)S(1)}, u32[]{:S(2)}, u32[]{:S(2)}) async-start(bf16[32,248,128]{2,1,0:T(8,128)(2,1)} %get-tuple-element.34), calls=%async_computation | async-start | bytes 4063232 | tf_op jit(solution)/shard_map/all_to_all | solution.py:562
  84.6 6.7 %collective-permute-start.4 = (f32[16,128]{1,0:T(8,128)S(1)}, f32[16,128]{1,0:T(8,128)S(1)}, u32[]{:S(2)}, u32[]{:S(2)}) collective-permute-start(f32[16,128]{1,0:T(8,128)S(1)} %get-tuple-element.41), channel_id=1, source_target_pairs={{0,8},{8,0},{16,24},{24,16},{1,9},{9,1},{17,25},{25,17},{2,10},{10... | collective-permute-start | bytes 24584 | tf_op jit(solution)/shard_map/ppermute | solution.py:47
  85.5 5.8 %collective-permute-start.5 = (f32[16,128]{1,0:T(8,128)S(1)}, f32[16,128]{1,0:T(8,128)S(1)}, u32[]{:S(2)}, u32[]{:S(2)}) collective-permute-start(f32[16,128]{1,0:T(8,128)S(1)} %get-tuple-element.42), channel_id=1, source_target_pairs={{8,16},{16,8},{9,17},{17,9},{10,18},{18,10},{11,19},{19,11},{12,20... | collective-permute-start | bytes 24584 | tf_op jit(solution)/shard_map/ppermute | solution.py:47

commit v5 on v4

--- a/solution.py
+++ b/solution.py
@@ -156,22 +156,22 @@
     return before, after
 
 
-def filter_planes(tiles, radar, left, right, planes):
+def filter_planes(tiles, radar, halo, planes):
     inner = pl.ds(SUB, tiles)
     blank = jnp.zeros((1, LANES), F32)
     for plane in range(3 + COMPS):
         planes[plane, SUB - 1 : SUB, :] = blank
         planes[plane, SUB + tiles : SUB + tiles + 1, :] = blank
-    squares = lambda values: sum(v * v for v in values)
-    lefts = [left[:, c : c + 1] for c in range(COMPS)]
-    rights = [right[:, c : c + 1] for c in range(COMPS)]
     total = jnp.zeros((tiles, LANES), F32)
+    beside = jnp.zeros((tiles, LANES), F32)
     for c in range(COMPS):
         x = radar[c].astype(F32)
+        side = halo[:, c * LANES : (c + 1) * LANES]
         total = total + x * x
-        before, after = with_sides(x, lefts[c], rights[c])
+        beside = beside + side * side
+        before, after = neighbours(x, side)
         planes[3 + c, inner, :] = x + before + after
-    for plane, value in enumerate((total,) + with_sides(total, squares(lefts), squares(rights))):
+    for plane, value in enumerate((total,) + neighbours(total, beside)):
         planes[plane, inner, :] = value
 
 
@@ -208,7 +208,10 @@
         edge_lines[band, 0] = radar[:, 0:tall, :]
         edge_lines[band, 1] = radar[:, z.lines[band] - tall :, :]
     after, before = by_parity("swath", swap_a[...].astype(F32), swap_b[...].astype(F32))
-    left, right = before.T, after.T
+    sides = jnp.concatenate([before, after], axis=0).astype(BF16)
+    column, to = iota((2 * SUB, COMPS * LANES), 0), iota((2 * SUB, COMPS * LANES), 1)
+    target = jnp.where(column < SUB, column * LANES + LANES - 1, (column - SUB) * LANES)
+    target = ones_where((to == target) & (column % SUB < COMPS))
     bands = (
         (radar_l, base_l, held_l, planes_l, filtered_l),
         (radar_s, base_s, weights_s, planes_s, filtered_s),
@@ -217,7 +220,7 @@
     for band in (1, 0):
         radar, _, _, planes, _ = bands[band]
         part = slice(at[band], at[band] + z.lines[band])
-        filter_planes(z.lines[band], radar, left[part], right[part], planes)
+        filter_planes(z.lines[band], radar, dot(sides[:, part], target, TN), planes)
     todo = [(band, start) for band in (1, 0) for start in range(0, z.lines[band], z.part)]
 
     def lines_of(band, start):
@@ -430,14 +433,18 @@
     return result[0 : n_model * SUB] + result[n_model * SUB :]
 
 
-def three_lanes(x, side):
+def neighbours(x, side):
     lane = iota(x.shape, 1)
     before = pltpu.roll(jnp.where(lane == LANES - 1, side, x), 1, 1)
-    after = pltpu.roll(jnp.where(lane == 0, side, x), LANES - 1, 1)
+    return before, pltpu.roll(jnp.where(lane == 0, side, x), LANES - 1, 1)
+
+
+def three_lanes(x, side):
+    before, after = neighbours(x, side)
     return x + before + after
 
 
-def spread_kernel(z, maps, planes, wide, out, ends, fits):
+def spread_kernel(z, maps, planes, wide, out, ends, fits, done, leaving):
     map_lines, n_model = z.map_lines, z.n_model
     for i in range(map_lines // (2 * SUB)):
         starts = (2 * i * SUB, (2 * i + 1) * SUB)
@@ -449,15 +456,20 @@
                 ]
     blank = jnp.zeros((1, LANES), F32)
     inner = pl.ds(SUB, map_lines)
+    copies = []
     for k in range(n_model):
         x = three_lanes(fits[k, inner, :], planes[:, k * LANES : (k + 1) * LANES])
         fits[k, inner, :] = x
         fits[k, SUB - 1 : SUB, :] = blank
         fits[k, SUB + map_lines : SUB + map_lines + 1, :] = blank
         x = fits[k, pl.ds(SUB - 1, map_lines), :] + x + fits[k, pl.ds(SUB + 1, map_lines), :]
-        out[k] = x
+        done[k] = x
+        copies.append(pltpu.make_async_copy(done.at[k], out.at[k], leaving.at[k]))
+        copies[-1].start()
         ends[0, k] = x[0:SUB]
         ends[1, k] = x[map_lines - SUB :]
+    for copy in copies:
+        copy.wait()
 
 
 def finish_kernel(z, given, ends, sec_a, sec_b, out, held, moving):
@@ -479,11 +491,11 @@
     lines_l, lines_s = z.lines
     shape = jax.ShapeDtypeStruct
 
-    def call(kernel, args, shapes, mib, scratch=(), specs=None, flops=0, size=0):
+    def call(kernel, args, shapes, mib, scratch=(), specs=None, outs=None, flops=0, size=0):
         return pl.pallas_call(
             lambda *refs: kernel(z, *refs) if kernel is not matrix_kernel else kernel(*refs),
             in_specs=specs or [VMEM] * len(args),
-            out_specs=[VMEM] * len(shapes),
+            out_specs=outs or [VMEM] * len(shapes),
             out_shape=shapes,
             scratch_shapes=scratch,
             compiler_params=params(mib),
@@ -593,7 +605,12 @@
         (maps, planes, wide),
         [shape((z.n_model, z.map_lines, LANES), F32), edge],
         24,
-        scratch=[pltpu.VMEM((z.n_model, z.map_lines + 2 * SUB, LANES), F32)],
+        scratch=[
+            pltpu.VMEM((z.n_model, z.map_lines + 2 * SUB, LANES), F32),
+            pltpu.VMEM((z.n_model, z.map_lines, LANES), F32),
+            pltpu.SemaphoreType.DMA((z.n_model,)),
+        ],
+        outs=[ANY, VMEM],
         flops=10_000_000_000,
         size=4_000_000,
     )

time: 92.2 us -> 91 us (0.987)
  Pallas kernels: 24.8 us -> 23.5 us
    pallas_call x4, Pallas kernels: 18.3 us -> 17 us  [call(): pl.pallas_call(lambda *refs: kernel(z, *refs) if kernel is not matrix_ker...]
  transfers between devices with their start and end apart: 7 -> 7, of which waited for: 2 -> 2; matrix products, arithmetic and copies ran while one was open for 0% -> 0% of each run, Pallas kernels for 17% -> 16%
where the time goes in v5:
time: 91 us; the launch traced here: 90.7 us
  waiting for transfers between devices  46.7 us (51%)
  Pallas kernels  23.5 us (26%)
  starting transfers between devices  20.2 us (22%)
    all_to_all x1, waiting for transfers between devices, body(): got = lax.all_to_all(sent, AXES, split_axis=0, concat_axis=0, tiled=True)  46.1 us
    pallas_call x4, Pallas kernels, call(): pl.pallas_call(lambda *refs: kernel(z, *refs) if kernel is not matrix_ker...  17 us
    all_to_all x1, starting transfers between devices, body(): got = lax.all_to_all(sent, AXES, split_axis=0, concat_axis=0, tiled=True)  8.85 us
    ppermute x3, starting transfers between devices, swap(): lax.ppermute(odd_pairs, axis, pairs(1))  6.78 us
    ppermute x3, starting transfers between devices, swap(): lax.ppermute(even_pairs, axis, pairs(0))  4.6 us
    pallas_call x2, Pallas kernels, call_one(): pl.pallas_call(lambda *refs: kernel(z, *refs), grid=(1,), in_specs=specs,...  3.17 us
    pallas_call x1, Pallas kernels, body(): pl.pallas_call(lambda *refs: tail_kernel(z, *refs), in_specs=[SMEM, SMEM]...  2.61 us
  transfers between devices with their start and end apart: 7, of which 2 were waited for; matrix products, arithmetic and copies ran while one was open for 0% of the time, Pallas kernels for 16%

profile of v5, /device:TPU:1, one launch (start us, length us, event | category | flops | bytes accessed | tf_op | source)
XLA Modules:
  0.0 90.7 jit_solution(16080638725514172804)
XLA Ops:
  0.0 3.1 %shard_map.91 = (bf16[8,640]{1,0:T(8,128)(2,1)}, bf16[8,640]{1,0:T(8,128)(2,1)}, s32[1,384]{1,0:T(1,128)}, s32[1,256]{1,0:T(1,128)}, f32[32,128]{1,0:T(8,128)}) custom-call(bf16[6,384,128]{2,1,0:T(8,128)(2,1)} %refs_2_.3, bf16[6,256,128]{2,1,0:T(8,128)(2,1)} %refs_3_.5, s32[1,384]{1,0:T(1,128)} %bitcast.2, s32[384]{0:T(512)} %refs_3_.3, s32[1,256]{1,0:T(1,128)} %bitcast.3, ...), custom_call_target="tpu_custom_call" | custom-call | flops 10000000000 | bytes 1000000 | tf_op jit(solution)/shard_map/pallas_call | solution.py:506
  3.1 2.1 %collective-permute-start = (bf16[8,640]{1,0:T(8,128)(2,1)}, bf16[8,640]{1,0:T(8,128)(2,1)S(1)}, u32[]{:S(2)}, u32[]{:S(2)}) collective-permute-start(bf16[8,640]{1,0:T(8,128)(2,1)} %get-tuple-element.26), channel_id=1, source_target_pairs={{0,1},{1,0},{2,3},{3,2},{4,5},{5,4},{6,7},{7,6},{8,9},{9,8},{10,11... | collective-permute-start | bytes 30728 | tf_op jit(solution)/shard_map/ppermute | solution.py:47
  5.2 0.7 collective-permute-start.1
  5.9 0.6 collective-permute-done.refs_4_.refs_5_
  6.5 0.0 collective-permute-done.1.refs_5_.refs_6_
  6.5 0.0 copy-start.3
  6.5 0.1 shard_map.93
  6.6 1.6 %collective-permute-start.2 = (bf16[40,128]{1,0:T(8,128)(2,1)S(1)}, bf16[40,128]{1,0:T(8,128)(2,1)S(1)}, u32[]{:S(2)}, u32[]{:S(2)}) collective-permute-start(bf16[40,128]{1,0:T(8,128)(2,1)S(1)} %get-tuple-element.29), channel_id=1, source_target_pairs={{0,8},{8,0},{16,24},{24,16},{1,9},{9,1},{17,25},{25,17},{2,10},{10... | collective-permute-start | bytes 30728 | tf_op jit(solution)/shard_map/ppermute | solution.py:47
  8.2 3.8 %collective-permute-start.3 = (bf16[40,128]{1,0:T(8,128)(2,1)S(1)}, bf16[40,128]{1,0:T(8,128)(2,1)S(1)}, u32[]{:S(2)}, u32[]{:S(2)}) collective-permute-start(bf16[40,128]{1,0:T(8,128)(2,1)S(1)} %get-tuple-element.30), channel_id=1, source_target_pairs={{8,16},{16,8},{9,17},{17,9},{10,18},{18,10},{11,19},{19,11},{12,20... | collective-permute-start | bytes 30728 | tf_op jit(solution)/shard_map/ppermute | solution.py:47
  12.0 0.0 copy-start
  12.0 9.7 %shard_map.92 = (f32[8336,128]{1,0:T(8,128)S(1)}, bf16[2,2,6,16,128]{4,3,2,1,0:T(8,128)(2,1)S(1)}, bf16[2,2,128,128]{3,2,1,0:T(8,128)(2,1)S(1)}) custom-call(s32[1,384]{1,0:T(1,128)S(1)} %copy-done.1, s32[1,256]{1,0:T(1,128)S(1)} %copy-done.2, bf16[6,384,128]{2,1,0:T(8,128)(2,1)S(1)} %copy-done.4, bf16[6,256,128]{2,1,0:T(8,128)(2,1)S(1)} %copy-done.5, ...), custom_call_target="tpu_custom_call" | custom-call | flops 10000000000 | bytes 20971520 | tf_op jit(solution)/shard_map/pallas_call | solution.py:495
  21.8 0.0 collective-permute-done.3.refs_4_
  21.8 2.6 %shard_map.94 = (bf16[32,248,128]{2,1,0:T(8,128)(2,1)}, f32[8336,128]{1,0:T(8,128)S(1)}) custom-call(s32[1,384]{1,0:T(1,128)S(1)} %copy-done.1, s32[1,256]{1,0:T(1,128)S(1)} %copy-done.2, f32[8336,128]{1,0:T(8,128)S(1)} %get-tuple-element.28.refs_2_, bf16[40,128]{1,0:T(8,128)(2,1)S(1)} %collective-permute-done.2.refs_3_, ...), custom_call_target="tpu_custom_call", output_to_operand_aliasing={{1}: (2, {})} | custom-call | tf_op jit(solution)/shard_map/pallas_call | solution.py:565
  24.4 0.0 copy-start.6
  24.4 8.8 %all-to-all-start = ((bf16[32,248,128]{2,1,0:T(8,128)(2,1)}), bf16[32,248,128]{2,1,0:T(8,128)(2,1)S(1)}, u32[]{:S(2)}, u32[]{:S(2)}) async-start(bf16[32,248,128]{2,1,0:T(8,128)(2,1)} %get-tuple-element.34), calls=%async_computation | async-start | bytes 4063232 | tf_op jit(solution)/shard_map/all_to_all | solution.py:574
  33.3 1.9 %shard_map.95 = (f32[16,36]{1,0:T(8,128)S(1)}, bf16[256,288]{1,0:T(8,128)(2,1)S(1)}) custom-call(f32[16,36]{1,0:T(8,128)S(1)} %copy-done.6), custom_call_target="tpu_custom_call" | custom-call | flops 50000000 | bytes 1000000 | tf_op jit(solution)/shard_map/pallas_call | solution.py:495
  35.2 46.1 %all-to-all-done.refs_0_ = bf16[32,248,128]{2,1,0:T(8,128)(2,1)S(1)} async-done(((bf16[32,248,128]{2,1,0:T(8,128)(2,1)}), bf16[32,248,128]{2,1,0:T(8,128)(2,1)S(1)}, u32[]{:S(2)}, u32[]{:S(2)}) %all-to-all-start) | async-done | bytes 2031648 | tf_op jit(solution)/shard_map/all_to_all | solution.py:574
  81.3 2.3 %shard_map.96 = (f32[12,256,128]{2,1,0:T(8,128)S(1)}, f32[256,2048]{1,0:T(8,128)S(1)}, f32[16,128]{1,0:T(8,128)S(1)}, f32[16,128]{1,0:T(8,128)S(1)}) custom-call(bf16[32,248,128]{2,1,0:T(8,128)(2,1)S(1)} %all-to-all-done.refs_0_, f32[16,36]{1,0:T(8,128)S(1)} %get-tuple-element.35.refs_1_, bf16[256,288]{1,0:T(8,128)(2,1)S(1)} %get-tuple-element.36.refs_2_), custom_call_target="tpu_custom_call" | custom-call | flops 1000000000 | bytes 4000000 | tf_op jit(solution)/shard_map/pallas_call | solution.py:495
  83.6 0.9 %collective-permute-start.4 = (f32[16,128]{1,0:T(8,128)S(1)}, f32[16,128]{1,0:T(8,128)S(1)}, u32[]{:S(2)}, u32[]{:S(2)}) collective-permute-start(f32[16,128]{1,0:T(8,128)S(1)} %get-tuple-element.41), channel_id=1, source_target_pairs={{0,8},{8,0},{16,24},{24,16},{1,9},{9,1},{17,25},{25,17},{2,10},{10... | collective-permute-start | bytes 24584 | tf_op jit(solution)/shard_map/ppermute | solution.py:47
  84.6 2.3 %collective-permute-start.5 = (f32[16,128]{1,0:T(8,128)S(1)}, f32[16,128]{1,0:T(8,128)S(1)}, u32[]{:S(2)}, u32[]{:S(2)}) collective-permute-start(f32[16,128]{1,0:T(8,128)S(1)} %get-tuple-element.42), channel_id=1, source_target_pairs={{8,16},{16,8},{9,17},{17,9},{10,18},{18,10},{11,19},{19,11},{12,20... | collective-permute-start | bytes 24584 | tf_op jit(solution)/shard_map/ppermute | solution.py:47
  86.9 3.1 %shard_map.97 = (f32[16,256,128]{2,1,0:T(8,128)}, f32[2,16,8,128]{3,2,1,0:T(8,128)S(1)}) custom-call(f32[12,256,128]{2,1,0:T(8,128)S(1)} %get-tuple-element.37.refs_0_, f32[256,2048]{1,0:T(8,128)S(1)} %get-tuple-element.38.refs_1_, bf16[256,288]{1,0:T(8,128)(2,1)S(1)} %get-tuple-element.36.refs_2_), custom_call_target="tpu_custom_call" | custom-call | flops 10000000000 | bytes 4000000 | tf_op jit(solution)/shard_map/pallas_call | solution.py:495
  90.0 0.0 collective-permute-done.4.refs_2_
  90.0 0.0 collective-permute-done.5.refs_3_
  90.0 0.7 shard_map.98
  (12 shorter events, 0.0 us)
Async XLA Ops:
  0.0 6.5 %copy-start.4 = (bf16[6,384,128]{2,1,0:T(8,128)(2,1)S(1)}, bf16[6,384,128]{2,1,0:T(8,128)(2,1)}, u32[]{:S(2)}) copy-start(bf16[6,384,128]{2,1,0:T(8,128)(2,1)} %refs_2_.3) | copy-start | bytes 1769476
  0.0 6.5 %copy-start.5 = (bf16[6,256,128]{2,1,0:T(8,128)(2,1)S(1)}, bf16[6,256,128]{2,1,0:T(8,128)(2,1)}, u32[]{:S(2)}) copy-start(bf16[6,256,128]{2,1,0:T(8,128)(2,1)} %refs_3_.5) | copy-start | bytes 1179652
  3.1 3.4 %collective-permute-start = (bf16[8,640]{1,0:T(8,128)(2,1)}, bf16[8,640]{1,0:T(8,128)(2,1)S(1)}, u32[]{:S(2)}, u32[]{:S(2)}) collective-permute-start(bf16[8,640]{1,0:T(8,128)(2,1)} %get-tuple-element.26), channel_id=1, source_target_pairs={{0,1},{1,0},{2,3},{3,2},{4,5},{5,4},{6,7},{7,6},{8,9},{9,8},{10,11... | collective-permute-start | bytes 30728 | tf_op jit(solution)/shard_map/ppermute | solution.py:47
  5.2 1.3 %collective-permute-start.1 = (bf16[8,640]{1,0:T(8,128)(2,1)}, bf16[8,640]{1,0:T(8,128)(2,1)S(1)}, u32[]{:S(2)}, u32[]{:S(2)}) collective-permute-start(bf16[8,640]{1,0:T(8,128)(2,1)} %get-tuple-element.27), channel_id=1, source_target_pairs={{1,2},{2,1},{3,4},{4,3},{5,6},{6,5},{9,10},{10,9},{11,12},{12,11},... | collective-permute-start | bytes 30728 | tf_op jit(solution)/shard_map/ppermute | solution.py:47
  6.5 5.5 %copy-start.1 = (s32[1,384]{1,0:T(1,128)S(1)}, s32[1,384]{1,0:T(1,128)}, u32[]{:S(2)}) copy-start(s32[1,384]{1,0:T(1,128)} %get-tuple-element.24.refs_0_) | copy-start | bytes 4612
  6.5 5.5 %copy-start.2 = (s32[1,256]{1,0:T(1,128)S(1)}, s32[1,256]{1,0:T(1,128)}, u32[]{:S(2)}) copy-start(s32[1,256]{1,0:T(1,128)} %get-tuple-element.25.refs_1_) | copy-start | bytes 3076
  6.5 5.5 %copy-start.3 = (bf16[256,128,128]{2,1,0:T(8,128)(2,1)S(1)}, bf16[256,128,128]{2,1,0:T(8,128)(2,1)}, u32[]{:S(2)}) copy-start(bf16[256,128,128]{2,1,0:T(8,128)(2,1)} %refs_7_.1) | copy-start | bytes 25165828
  6.6 15.1 %collective-permute-start.2 = (bf16[40,128]{1,0:T(8,128)(2,1)S(1)}, bf16[40,128]{1,0:T(8,128)(2,1)S(1)}, u32[]{:S(2)}, u32[]{:S(2)}) collective-permute-start(bf16[40,128]{1,0:T(8,128)(2,1)S(1)} %get-tuple-element.29), channel_id=1, source_target_pairs={{0,8},{8,0},{16,24},{24,16},{1,9},{9,1},{17,25},{25,17},{2,10},{10... | collective-permute-start | bytes 30728 | tf_op jit(solution)/shard_map/ppermute | solution.py:47
  8.2 13.6 %collective-permute-start.3 = (bf16[40,128]{1,0:T(8,128)(2,1)S(1)}, bf16[40,128]{1,0:T(8,128)(2,1)S(1)}, u32[]{:S(2)}, u32[]{:S(2)}) collective-permute-start(bf16[40,128]{1,0:T(8,128)(2,1)S(1)} %get-tuple-element.30), channel_id=1, source_target_pairs={{8,16},{16,8},{9,17},{17,9},{10,18},{18,10},{11,19},{19,11},{12,20... | collective-permute-start | bytes 30728 | tf_op jit(solution)/shard_map/ppermute | solution.py:47
  12.0 9.8 %copy-start = (f32[32,128]{1,0:T(8,128)S(1)}, f32[32,128]{1,0:T(8,128)}, u32[]{:S(2)}) copy-start(f32[32,128]{1,0:T(8,128)} %get-tuple-element.31.refs_7_) | copy-start | bytes 49156
  24.4 8.9 %copy-start.6 = (f32[16,36]{1,0:T(8,128)S(1)}, f32[16,36]{1,0:T(8,128)}, u32[]{:S(2)}) copy-start(f32[16,36]{1,0:T(8,128)} %refs_0_.5) | copy-start | bytes 6916
  24.4 56.9 %all-to-all-start = ((bf16[32,248,128]{2,1,0:T(8,128)(2,1)}), bf16[32,248,128]{2,1,0:T(8,128)(2,1)S(1)}, u32[]{:S(2)}, u32[]{:S(2)}) async-start(bf16[32,248,128]{2,1,0:T(8,128)(2,1)} %get-tuple-element.34), calls=%async_computation | async-start | bytes 4063232 | tf_op jit(solution)/shard_map/all_to_all | solution.py:574
  83.6 6.3 %collective-permute-start.4 = (f32[16,128]{1,0:T(8,128)S(1)}, f32[16,128]{1,0:T(8,128)S(1)}, u32[]{:S(2)}, u32[]{:S(2)}) collective-permute-start(f32[16,128]{1,0:T(8,128)S(1)} %get-tuple-element.41), channel_id=1, source_target_pairs={{0,8},{8,0},{16,24},{24,16},{1,9},{9,1},{17,25},{25,17},{2,10},{10... | collective-permute-start | bytes 24584 | tf_op jit(solution)/shard_map/ppermute | solution.py:47
  84.6 5.4 %collective-permute-start.5 = (f32[16,128]{1,0:T(8,128)S(1)}, f32[16,128]{1,0:T(8,128)S(1)}, u32[]{:S(2)}, u32[]{:S(2)}) collective-permute-start(f32[16,128]{1,0:T(8,128)S(1)} %get-tuple-element.42), channel_id=1, source_target_pairs={{8,16},{16,8},{9,17},{17,9},{10,18},{18,10},{11,19},{19,11},{12,20... | collective-permute-start | bytes 24584 | tf_op jit(solution)/shard_map/ppermute | solution.py:47
